TPU v7x, 256 devices: a whole 4x4x8 slice. The times are simulated.
256 devices in a mesh: dp: 64 (over x, z, core), mp: 4 (over y).
Axes of the slice: x: 4, y: 4, z: 8, core: 2. Of those that a mesh axis runs over, the one named last changes fastest.
Arguments:
- history: bfloat16 [1024, 32, 1024], P('dp', None, 'mp'), may hold values from -6 to 6
- lengths: int32 [1024], replicated, may hold values from 1 to 32, 16384 in all
- source: int32 [1024], replicated, may hold values from 0 to 1023, as said below
- owners: int32 [32768, 8], P(('dp', 'mp')), may hold values from 0 to 255, all different within a row; in each aligned block of 128 rows (0 to 127, 128 to 255, ...) at most 6 rows name the same one
- item_rows: int32 [32768, 8], P(('dp', 'mp')), may hold values from 0 to 511
- catalogue: bfloat16 [131072, 1024], P(('dp', 'mp')), may hold values from -6 to 6
- w_in: bfloat16 [4, 1024, 1024], P(None, None, 'mp'), may hold values from -0.1875 to 0.1875
- w_out: bfloat16 [1024, 1024], P('mp'), may hold values from -0.1875 to 0.1875
Outputs:
- w_in_grad: float32 [4, 1024, 1024], P(None, 'dp', 'mp')
- w_out_grad: float32 [1024, 1024], P('mp', 'dp')
- cat_grad: float32 [131072, 1024], P(('dp', 'mp'))
Inputs may be any that keep to these rules, and one draw needn't show every extreme that they name: `source`: a permutation; balanced slot k lies on index k // 16 of dp, and the 16 histories that start on one index of dp go to one index of dp at most (16 + 64 - 1) // 64 at a time, that many for some index. Each event names 8 different owners, column 0 the positive item's; the events of one device (aligned blocks of 128) name one owner at most 6 times.
All inputs are finite; a program needn't handle non-finite values.
Results may differ from a plain program's by a relative error of at most 0.017.
Values may be sent and summed in bfloat16 or wider, within the bound.
A program may use at most 128 MiB of HBM per device.

v0:
```python
import jax
import jax.numpy as jnp
from jax import lax
from jax.sharding import PartitionSpec as P

DH = 128


cosine_divisor = 0.05
epsilon_norm = 1e-05
epsilon_unit = 1e-06


def normalize(rows_in):
    centered = rows_in - jnp.mean(rows_in, axis=-1, keepdims=True)
    spread = jnp.mean(centered * centered, axis=-1, keepdims=True)
    return centered / jnp.sqrt(spread + epsilon_norm)


def attend(projected, length_here):
    gating = projected[0]
    values = projected[1]
    queries = projected[2]
    key_rows = projected[3]
    steps_n = projected.shape[1]
    scores = jnp.einsum(
        "thd,shd->hts", queries, key_rows, preferred_element_type=jnp.float32
    ) / jnp.sqrt(jnp.float32(projected.shape[3]))
    places = jnp.arange(steps_n, dtype=jnp.int32)
    allowed = (places[None, :] <= places[:, None]) & (places[None, :] < length_here)
    weights = jnp.where(
        allowed[None], jax.nn.silu(scores) / length_here.astype(jnp.float32), 0.0
    ).astype(jnp.bfloat16)
    mixed_out = jnp.einsum("hts,shd->thd", weights, values, preferred_element_type=jnp.float32)
    return (normalize(mixed_out) * gating.astype(jnp.float32)).astype(jnp.bfloat16)


def loss_block(out_rows, valid_rows, fetched):
    out_norm = jnp.sqrt(jnp.sum(out_rows * out_rows, axis=-1, keepdims=True) + epsilon_unit)
    request_unit_vector = out_rows / out_norm
    item_f = fetched.astype(jnp.float32)
    item_norm = jnp.sqrt(jnp.sum(item_f * item_f, axis=-1, keepdims=True) + epsilon_unit)
    catalog_unit_vector = item_f / item_norm
    cosine_match_raw = (
        jnp.einsum("qn,qgn->qg", request_unit_vector, catalog_unit_vector) / cosine_divisor
    )
    expo = jnp.exp(cosine_match_raw)
    probs = expo / jnp.sum(expo, axis=-1, keepdims=True)
    column = jnp.arange(cosine_match_raw.shape[1], dtype=jnp.int32)
    exponent_shares = (probs - (column[None, :] == 0).astype(jnp.float32)) * valid_rows[
        :, None
    ].astype(jnp.float32)
    request_unit_vector_slope = (
        jnp.einsum("as,asy->ay", exponent_shares, catalog_unit_vector) / cosine_divisor
    )
    out_grad = (
        request_unit_vector_slope
        - request_unit_vector
        * jnp.sum(request_unit_vector * request_unit_vector_slope, axis=-1, keepdims=True)
    ) / out_norm
    catalog_unit_vector_slope = (
        exponent_shares[:, :, None] * request_unit_vector[:, None, :] / cosine_divisor
    )
    item_grad = (
        catalog_unit_vector_slope
        - catalog_unit_vector
        * jnp.sum(catalog_unit_vector * catalog_unit_vector_slope, axis=-1, keepdims=True)
    ) / item_norm
    return (out_grad, item_grad)


def silu_slope(preact):
    sigma = jax.nn.sigmoid(preact)
    return sigma * (1.0 + preact * (1.0 - sigma))


def earlier_same(labels):
    order_ids = jnp.arange(labels.shape[0], dtype=jnp.int32)
    same = (labels[None, :] == labels[:, None]) & (order_ids[None, :] < order_ids[:, None])
    return jnp.sum(same.astype(jnp.int32), axis=1)


def per_device(history, lengths, source, owners, item_rows, catalogue, w_in, w_out):
    dp_count = lax.axis_size("dp")
    mp_count = lax.axis_size("mp")
    dev_count = dp_count * mp_count
    here_dp = lax.axis_index("dp")
    here_mp = lax.axis_index("mp")
    seq_dev, steps_n, cols_here = history.shape
    seq_total = source.shape[0]
    per_peer = (seq_dev + dp_count - 1) // dp_count
    target = (
        jnp.zeros((seq_total,), jnp.int32).at[source].set(jnp.arange(seq_total, dtype=jnp.int32))
    )
    slot_ids = jnp.arange(seq_dev, dtype=jnp.int32)
    my_seqs = here_dp * seq_dev + slot_ids
    dest_dev = target[my_seqs] // seq_dev
    send_rank = earlier_same(dest_dev)
    outgoing = (
        jnp.zeros((dp_count, per_peer, steps_n, cols_here), jnp.bfloat16)
        .at[dest_dev, send_rank]
        .set(history)
    )
    arrived = lax.all_to_all(outgoing, "dp", split_axis=0, concat_axis=0, tiled=True)
    taken = source[my_seqs]
    anchor = taken // seq_dev
    anchor_block = anchor[:, None] * seq_dev + slot_ids[None, :]
    goes_here = target[anchor_block] // seq_dev == here_dp
    earlier = slot_ids[None, :] < (taken % seq_dev)[:, None]
    recv_rank = jnp.sum((goes_here & earlier).astype(jnp.int32), axis=1)
    counts = lengths[taken]
    local_rows = jnp.take(
        arrived.reshape(dp_count * per_peer, steps_n, cols_here),
        anchor * per_peer + recv_rank,
        axis=0,
    )
    features = lax.all_gather(local_rows, "mp", axis=2, tiled=True)
    rows_all = seq_dev * steps_n
    width = features.shape[2]
    flat_rows = features.reshape(rows_all, width)
    normed = normalize(flat_rows.astype(jnp.float32)).astype(jnp.bfloat16)
    preact = jnp.einsum("rd,cdh->crh", normed, w_in, preferred_element_type=jnp.float32)
    projected = jax.nn.silu(preact).astype(jnp.bfloat16)
    cols_heads = w_in.shape[2]
    heads_here = cols_heads // DH
    grouped = projected.reshape(4, seq_dev, steps_n, heads_here, DH)

    def run_all(inputs):
        return jax.vmap(attend, in_axes=(1, 0))(inputs, counts)

    gated, back = jax.vjp(run_all, grouped)
    gated_flat = gated.reshape(rows_all, cols_heads)
    partial_out = jnp.dot(gated_flat, w_out, preferred_element_type=jnp.float32)
    quarter = rows_all // mp_count
    summed = lax.psum(partial_out, "mp")
    out_rows = lax.dynamic_slice_in_dim(summed, here_mp * quarter, quarter, 0)
    out_rows = out_rows + lax.dynamic_slice_in_dim(flat_rows, here_mp * quarter, quarter, 0).astype(
        jnp.float32
    )
    position = here_mp * quarter + jnp.arange(quarter, dtype=jnp.int32)
    valid_rows = position % steps_n < counts[position // steps_n]
    top_n = owners.shape[1]
    asks = quarter * top_n
    capacity = max(2, (3 * asks + 2 * dev_count - 1) // (2 * dev_count))
    owner_flat = owners.reshape(-1)
    row_flat = item_rows.reshape(-1)
    rank_in = earlier_same(owner_flat)
    address = owner_flat * capacity + rank_in
    slot_table = (
        jnp.full((dev_count * capacity,), asks, jnp.int32)
        .at[address]
        .set(jnp.arange(asks, dtype=jnp.int32))
    )
    is_used = slot_table < asks
    safe_index = jnp.minimum(slot_table, asks - 1)
    wanted = jnp.where(is_used, row_flat[safe_index], 0).reshape(dp_count, mp_count, capacity)
    incoming = lax.all_to_all(
        lax.all_to_all(wanted, "dp", split_axis=0, concat_axis=0, tiled=True),
        "mp",
        split_axis=1,
        concat_axis=1,
        tiled=True,
    )
    incoming_flat = incoming.reshape(-1)
    looked = jnp.take(catalogue, incoming_flat, axis=0).reshape(dp_count, mp_count, capacity, width)
    returned = lax.all_to_all(
        lax.all_to_all(looked, "dp", split_axis=0, concat_axis=0, tiled=True),
        "mp",
        split_axis=1,
        concat_axis=1,
        tiled=True,
    )
    fetched = jnp.take(returned.reshape(dev_count * capacity, width), address, axis=0).reshape(
        quarter, top_n, width
    )
    out_grad, item_grad = loss_block(out_rows, valid_rows, fetched)
    item_flat = item_grad.reshape(asks, width)
    sending = jnp.where(is_used[:, None], jnp.take(item_flat, safe_index, axis=0), 0.0)
    landed = lax.all_to_all(
        lax.all_to_all(
            sending.reshape(dp_count, mp_count, capacity, width).astype(jnp.bfloat16),
            "dp",
            split_axis=0,
            concat_axis=0,
            tiled=True,
        ),
        "mp",
        split_axis=1,
        concat_axis=1,
        tiled=True,
    ).astype(jnp.float32)
    cat_grad = (
        jnp.zeros((catalogue.shape[0], width), jnp.float32)
        .at[incoming_flat]
        .add(landed.reshape(-1, width))
    )
    out_cotangent = lax.all_gather(out_grad.astype(jnp.bfloat16), "mp", axis=0, tiled=True)
    w_out_part = jnp.einsum(
        "rh,rd->hd", gated_flat, out_cotangent, preferred_element_type=jnp.float32
    )
    gated_cotangent = jnp.einsum(
        "rd,hd->rh", out_cotangent, w_out, preferred_element_type=jnp.float32
    ).astype(jnp.bfloat16)
    (grouped_cotangent,) = back(gated_cotangent.reshape(seq_dev, steps_n, heads_here, DH))
    projected_cotangent = grouped_cotangent.reshape(4, rows_all, cols_heads)
    preact_cotangent = (projected_cotangent.astype(jnp.float32) * silu_slope(preact)).astype(
        jnp.bfloat16
    )
    w_in_part = jnp.einsum(
        "rd,crh->cdh", normed, preact_cotangent, preferred_element_type=jnp.float32
    )
    w_in_grad, w_out_grad = (
        lax.psum_scatter(w_in_part, "dp", scatter_dimension=1, tiled=True),
        lax.psum_scatter(w_out_part, "dp", scatter_dimension=1, tiled=True),
    )
    return (w_in_grad, w_out_grad, cat_grad)


def solution(mesh):
    placed = (
        P("dp", None, "mp"),
        P(),
        P(),
        P(("dp", "mp"), None),
        P(("dp", "mp"), None),
        P(("dp", "mp"), None),
        P(None, None, "mp"),
        P("mp", None),
    )
    return jax.shard_map(
        per_device,
        mesh=mesh,
        in_specs=placed,
        out_specs=(P(None, "dp", "mp"), P("mp", "dp"), P(("dp", "mp"), None)),
        check_vma=False,
    )
```

profile of v0, /device:TPU:1, one launch (start us, length us, event | category | flops | bytes accessed | tf_op | source)
XLA Modules:
  0.0 683.9 jit_solution(856039338225278554)
XLA Ops:
  15.3 5.9 gather_fusion.5
  22.6 13.0 %all-to-all-start.1 = ((s32[64,4,6]{2,1,0:T(4,128)}), s32[64,4,6]{2,1,0:T(4,128)S(1)}, u32[]{:S(2)}, u32[]{:S(2)}) async-start(s32[64,4,6]{2,1,0:T(4,128)} %reshape.655), calls=%async_computation.1 | async-start | bytes 262144 | tf_op jit(solution)/shard_map/all_to_all | solution.py:158
  36.3 4.3 scatter_custom_fusion
  41.5 4.5 all-to-all-done.1
  55.1 8.0 %all-to-all-start = ((bf16[64,1,32,256]{3,2,1,0:T(8,128)(2,1)}), bf16[64,1,32,256]{3,2,1,0:T(8,128)(2,1)}, u32[]{:S(2)}, u32[]{:S(2)}) async-start(bf16[64,1,32,256]{3,2,1,0:T(8,128)(2,1)} %bitcast.239), calls=%async_computation | async-start | bytes 2097152 | tf_op jit(solution)/shard_map/all_to_all | solution.py:104
  65.0 5.8 gather_fusion.6
  70.8 6.2 gather.53
  79.7 7.9 %copy.116 = bf16[64,4,6,1024]{3,1,2,0:T(4,128)(2,1)} copy(bf16[64,4,6,1024]{3,2,1,0:T(8,128)(2,1)S(1)} %broadcast_select_fusion) | data formatting | bytes 6291456 | tf_op jit(solution)/shard_map/jit(_take)/select_n | solution.py:165
  91.3 6.7 all-to-all-start.3
  104.2 25.0 %all-gather.3.cloned.1.call-done = bf16[16,32,1024]{2,1,0:T(8,128)(2,1)} async-done(((bf16[16,32,256]{2,1,0:T(8,128)(2,1)}), bf16[16,32,1024]{2,1,0:T(8,128)(2,1)}) %all-gather.3.cloned.1.call-update) | async-done | bytes 1048592 | tf_op jit(solution)/shard_map/all_gather | solution.py:117
  141.1 30.3 %all-to-all-done.3 = bf16[64,4,6,1024]{3,1,2,0:T(4,128)(2,1)} async-done(((bf16[64,4,6,1024]{3,1,2,0:T(4,128)(2,1)}), bf16[64,4,6,1024]{3,1,2,0:T(4,128)(2,1)}, u32[]{:S(2)}, u32[]{:S(2)}) %all-to-all-start.3) | async-done | bytes 3145760 | tf_op jit(solution)/shard_map/all_to_all | solution.py:167
  171.4 5.3 copy.117
  186.7 10.0 %compare_convert_fusion = f32[128]{0:T(128)S(1)} fusion(s32[]{:T(128)} %bitcast.39, s32[]{:T(128)} %bitcast.40, s32[]{:T(128)} %bitcast.41, s32[]{:T(128)} %bitcast.42, s32[]{:T(128)} %bitcast.43, s32[]{:T(128)} %bitcast.45, s32[]{:T(128)} %bitcast.44, s32[]{:T(128)} %bitcast.22, s32[]{:T(128)} %bitcast.24, s32[]{:T(128)} %bitcast.26, s32[]{:T(128)} %bitcast.28, ...), kind=kLoop, calls=%fused_computation.196 | loop fusion | flops 8064 | bytes 580 | tf_op jit(solution)/shard_map/convert_element_type | solution.py:52
  198.1 25.9 %all-reduce.8.cloned.1.call-done = f32[512,1024]{1,0:T(8,128)} async-done(((f32[512,1024]{1,0:T(8,128)}), f32[512,1024]{1,0:T(8,128)}) %all-reduce.8.cloned.1.call-update) | async-done | bytes 2097168 | tf_op jit(solution)/shard_map/psum | solution.py:135
  227.3 8.0 %all-to-all-done.4 = bf16[64,4,6,1024]{3,0,2,1:T(8,128)(2,1)S(1)} async-done(((bf16[64,4,6,1024]{3,0,2,1:T(8,128)(2,1)}), bf16[64,4,6,1024]{3,0,2,1:T(8,128)(2,1)S(1)}, u32[]{:S(2)}, u32[]{:S(2)}) %all-to-all-start.4) | async-done | bytes 3145760 | tf_op jit(solution)/shard_map/all_to_all | solution.py:166
  239.0 4.9 reshape.657
  243.9 5.3 gather_fusion.7
  259.9 5.8 gather_fusion.8
  265.7 6.2 gather.58
  272.0 4.4 fusion.1
  280.6 5.6 all-to-all-start.5
  287.4 28.8 %all-gather.5.cloned.1.call-done = bf16[512,1024]{1,0:T(8,128)(2,1)} async-done(((bf16[128,1024]{1,0:T(8,128)(2,1)}), bf16[512,1024]{1,0:T(8,128)(2,1)}) %all-gather.5.cloned.1.call-update) | async-done | bytes 1048592 | tf_op jit(solution)/shard_map/all_gather | solution.py:197
  326.6 6.1 convolution_bitcast_fusion
  332.7 5.2 copy.129
  337.9 22.7 %all-to-all-done.5 = bf16[64,4,6,1024]{3,1,2,0:T(4,128)(2,1)} async-done(((bf16[64,4,6,1024]{3,1,2,0:T(4,128)(2,1)}), bf16[64,4,6,1024]{3,1,2,0:T(4,128)(2,1)}, u32[]{:S(2)}, u32[]{:S(2)}) %all-to-all-start.5) | async-done | bytes 3145760 | tf_op jit(solution)/shard_map/all_to_all | solution.py:180
  360.7 5.4 copy.134
  366.1 5.6 all-to-all-start.6
  375.8 161.2 %all-reduce.10.cloned.1.call-done = f32[4,1024,256]{2,0,1:T(4,128)} async-done(((f32[4,1024,256]{2,0,1:T(4,128)}), f32[4,1024,256]{2,0,1:T(4,128)}) %all-reduce.10.cloned.1.call-update) | async-done | bytes 4194320
  538.4 5.1 copy.135
  543.6 8.4 %reshape.790 = f32[1536,1024]{1,0:T(8,128)} reshape(f32[64,4,6,1024]{3,2,1,0:T(8,128)} %copy.135) | data formatting | bytes 12582912 | tf_op jit(solution)/shard_map/reshape | solution.py:195
  552.0 16.0 %scatter_custom_fusion.3 = f32[512,1024]{1,0:T(8,128)} fusion(s32[1536]{0:T(1024)} %copy-done.39, f32[1536,1024]{1,0:T(8,128)} %reshape.790, f32[]{:T(128)} %constant.182.clone.1), kind=kCustom, calls=%fused_computation.68 | custom fusion | flops 1572864 | bytes 2097664 | tf_op jit(solution)/shard_map/scatter-add | solution.py:195
  568.1 108.9 %reduce-scatter.2.cloned.1.call-done = f32[256,16]{0,1:T(8,128)} async-done(((f32[256,1024]{0,1:T(8,128)}), f32[256,16]{0,1:T(8,128)}) %reduce-scatter.2.cloned.1.call-update) | async-done | bytes 16400 | tf_op jit(solution)/shard_map/reduce_scatter | solution.py:214
  (235 shorter events, 95.4 us)
Async XLA Ops:
  7.2 125.4 %copy-start = (bf16[4,1024,256]{2,1,0:T(8,128)(2,1)S(1)}, bf16[4,1024,256]{2,1,0:T(8,128)(2,1)}, u32[]{:S(2)}) copy-start(bf16[4,1024,256]{2,1,0:T(8,128)(2,1)} %param.14) | copy-start | bytes 6291460
  9.3 5.1 copy-start.38
  14.4 6.8 copy-start.29
  14.4 6.8 copy-start.30
  15.3 20.4 %copy-start.3 = (s32[1024]{0:T(1024)S(1)}, s32[1024]{0:T(1024)}, u32[]{:S(2)}) copy-start(s32[1024]{0:T(1024)} %param.10) | copy-start | bytes 12292
  22.6 23.3 %all-to-all-start.1 = ((s32[64,4,6]{2,1,0:T(4,128)}), s32[64,4,6]{2,1,0:T(4,128)S(1)}, u32[]{:S(2)}, u32[]{:S(2)}) async-start(s32[64,4,6]{2,1,0:T(4,128)} %reshape.655), calls=%async_computation.1 | async-start | bytes 262144 | tf_op jit(solution)/shard_map/all_to_all | solution.py:158
  46.7 8.3 %all-to-all-start.2 = ((s32[4,1,384]{2,1,0:T(1,128)}), s32[4,1,384]{2,1,0:T(1,128)S(1)}, u32[]{:S(2)}, u32[]{:S(2)}) async-start(s32[4,1,384]{2,1,0:T(1,128)} %reshape.856), calls=%async_computation.2 | async-start | bytes 12288 | tf_op jit(solution)/shard_map/all_to_all | solution.py:157
  50.9 14.1 %copy-start.2 = (bf16[512,1024]{1,0:T(8,128)(2,1)S(1)}, bf16[512,1024]{1,0:T(8,128)(2,1)}, u32[]{:S(2)}) copy-start(bf16[512,1024]{1,0:T(8,128)(2,1)} %param.13) | copy-start | bytes 3145732
  55.1 36.2 %all-to-all-start = ((bf16[64,1,32,256]{3,2,1,0:T(8,128)(2,1)}), bf16[64,1,32,256]{3,2,1,0:T(8,128)(2,1)}, u32[]{:S(2)}, u32[]{:S(2)}) async-start(bf16[64,1,32,256]{3,2,1,0:T(8,128)(2,1)} %bitcast.239), calls=%async_computation | async-start | bytes 2097152 | tf_op jit(solution)/shard_map/all_to_all | solution.py:104
  65.0 5.9 copy-start.39
  91.3 80.1 %all-to-all-start.3 = ((bf16[64,4,6,1024]{3,1,2,0:T(4,128)(2,1)}), bf16[64,4,6,1024]{3,1,2,0:T(4,128)(2,1)}, u32[]{:S(2)}, u32[]{:S(2)}) async-start(bf16[64,4,6,1024]{3,1,2,0:T(4,128)(2,1)} %copy.116), calls=%async_computation.3 | async-start | bytes 6291456 | tf_op jit(solution)/shard_map/all_to_all | solution.py:167
  98.0 31.2 %all-gather.3.cloned.1.call-start = ((), (), s32[]{:S(2)}) async-start(), calls=%async_computation.8 | async-start | bytes 1310720 | tf_op jit(solution)/shard_map/all_gather | solution.py:117
  98.1 4.9 copy-start.4
  102.4 121.6 %all-reduce.8.cloned.1.call-start = ((), (), s32[]{:S(2)}) async-start(), calls=%async_computation.9 | async-start | bytes 4194304 | tf_op jit(solution)/shard_map/psum | solution.py:135
  103.7 32.3 %copy-start.47 = (f32[16]{0:T(128)}, f32[16]{0:T(128)S(1)}, u32[]{:S(2)}) copy-start(f32[16]{0:T(128)S(1)} %convert_element_type.130) | copy-start | bytes 196
  104.2 31.8 %copy-start.34 = (pred[16,32,32]{2,1,0:T(8,128)(4,1)}, pred[16,32,32]{2,1,0:T(8,128)(4,1)S(1)}, u32[]{:S(2)}) copy-start(pred[16,32,32]{2,1,0:T(8,128)(4,1)S(1)} %broadcast_and_fusion) | copy-start | bytes 49156
  129.2 3.4 copy-start.12
  130.8 4.6 copy-start.42
  137.2 3.9 copy-start.22
  176.7 58.5 %all-to-all-start.4 = ((bf16[64,4,6,1024]{3,0,2,1:T(8,128)(2,1)}), bf16[64,4,6,1024]{3,0,2,1:T(8,128)(2,1)S(1)}, u32[]{:S(2)}, u32[]{:S(2)}) async-start(bf16[64,4,6,1024]{3,0,2,1:T(8,128)(2,1)} %copy.117), calls=%async_computation.4 | async-start | bytes 6291456 | tf_op jit(solution)/shard_map/all_to_all | solution.py:166
  280.6 80.1 %all-to-all-start.5 = ((bf16[64,4,6,1024]{3,1,2,0:T(4,128)(2,1)}), bf16[64,4,6,1024]{3,1,2,0:T(4,128)(2,1)}, u32[]{:S(2)}, u32[]{:S(2)}) async-start(bf16[64,4,6,1024]{3,1,2,0:T(4,128)(2,1)} %copy.133), calls=%async_computation.6 | async-start | bytes 6291456 | tf_op jit(solution)/shard_map/all_to_all | solution.py:180
  286.2 30.0 %copy-start.15 = (bf16[256,1024]{1,0:T(8,128)(2,1)S(1)}, bf16[256,1024]{1,0:T(8,128)(2,1)}, u32[]{:S(2)}) copy-start(bf16[256,1024]{1,0:T(8,128)(2,1)} %param.15) | copy-start | bytes 1572868
  286.2 30.0 %all-gather.5.cloned.1.call-start = ((), (), s32[]{:S(2)}) async-start(), calls=%async_computation.10 | async-start | bytes 1310720 | tf_op jit(solution)/shard_map/all_gather | solution.py:197
  286.5 31.8 %copy-start.8 = (f32[16,32,2,128]{3,1,2,0:T(8,128)S(1)}, f32[16,32,2,128]{3,1,2,0:T(8,128)}, u32[]{:S(2)}) copy-start(f32[16,32,2,128]{3,1,2,0:T(8,128)} %copy-done.7) | copy-start | bytes 1572868
  286.5 31.8 %copy-start.11 = (f32[16,32,2,128]{3,2,1,0:T(2,128)S(1)}, f32[16,32,2,128]{3,2,1,0:T(2,128)}, u32[]{:S(2)}) copy-start(f32[16,32,2,128]{3,2,1,0:T(2,128)} %copy-done.10) | copy-start | bytes 1572868
  286.5 31.8 %copy-start.32 = (f32[16,32,2]{1,2,0:T(2,128)S(1)}, f32[16,32,2]{1,2,0:T(2,128)}, u32[]{:S(2)}) copy-start(f32[16,32,2]{1,2,0:T(2,128)} %get-tuple-element.29) | copy-start | bytes 12292
  287.4 31.5 %copy-start.28 = (f32[16,32,2]{1,2,0:T(2,128)S(1)}, f32[16,32,2]{1,2,0:T(2,128)}, u32[]{:S(2)}) copy-start(f32[16,32,2]{1,2,0:T(2,128)} %copy-done.27) | copy-start | bytes 12292
  287.4 31.5 %copy-start.26 = (f32[16,32,2]{1,2,0:T(2,128)S(1)}, f32[16,32,2]{1,2,0:T(2,128)}, u32[]{:S(2)}) copy-start(f32[16,32,2]{1,2,0:T(2,128)} %copy-done.25) | copy-start | bytes 12292
  287.4 249.6 %all-reduce.10.cloned.1.call-start = ((), (), s32[]{:S(2)}) async-start(), calls=%async_computation.12 | async-start | bytes 8388608
  366.1 172.4 %all-to-all-start.6 = ((bf16[64,4,6,1024]{3,0,2,1:T(8,128)(2,1)}), bf16[64,4,6,1024]{3,0,2,1:T(8,128)(2,1)S(1)}, u32[]{:S(2)}, u32[]{:S(2)}) async-start(bf16[64,4,6,1024]{3,0,2,1:T(8,128)(2,1)} %copy.134), calls=%async_computation.7 | async-start | bytes 6291456 | tf_op jit(solution)/shard_map/all_to_all | solution.py:179
  371.7 305.2 %reduce-scatter.2.cloned.1.call-start = ((), (), s32[]{:S(2)}) async-start(), calls=%async_computation.11 | async-start | bytes 1064960 | tf_op jit(solution)/shard_map/reduce_scatter | solution.py:214
  543.6 133.3 %copy-start.1 = (bf16[4,1024,256]{2,1,0:T(8,128)(2,1)S(1)}, bf16[4,1024,256]{2,1,0:T(8,128)(2,1)}, u32[]{:S(2)}) copy-start(bf16[4,1024,256]{2,1,0:T(8,128)(2,1)} %param.14) | copy-start | bytes 6291460
  (30 other events, 54.8 us)
Sparse Core Ops, SparseCore 0:
  102.5 26.6 all-gather.2
  141.3 82.6 all-reduce.7
  288.8 27.3 all-gather.4
  338.1 198.8 all-reduce.9
  541.4 135.5 reduce-scatter.1
where the time goes:
time: 695 us; the launch traced here: 684 us
  waiting for transfers between devices  419 us (60%)
  local copies, waits for them, and re-layouts  123 us (18%)
  other arithmetic  55.5 us (8%)
  starting transfers between devices  47.7 us (7%)
  matrix products  21.9 us (3%)
  between operations  16 us (2%)
    unnamed x6, waiting for transfers between devices  161 us
    reduce_scatter x1, waiting for transfers between devices, per_device(): lax.psum_scatter(w_out_part, 'dp', scatter_dimension=1, tiled=True)  109 us
    all_to_all x1, waiting for transfers between devices, per_device(): lax.all_to_all(looked, 'dp', split_axis=0, concat_axis=0, tiled=True)  30.3 us
    all_gather x1, waiting for transfers between devices, per_device(): lax.all_gather(out_grad.astype(jnp.bfloat16), 'mp', axis=0, tiled=True)  28.8 us
    psum x1, waiting for transfers between devices, per_device(): summed = lax.psum(partial_out, 'mp')  25.9 us
    all_gather x1, waiting for transfers between devices, per_device(): features = lax.all_gather(local_rows, 'mp', axis=2, tiled=True)  25 us
    all_to_all x1, waiting for transfers between devices, per_device(): lax.all_to_all(sending.reshape(dp_count, mp_count, capacity, width).astyp...  22.7 us
    scatter-add x1, other arithmetic, per_device(): cat_grad = jnp.zeros((catalogue.shape[0], width), jnp.float32).at[incomin...  16 us
  transfers between devices with their start and end apart: 12, of which 11 were waited for; matrix products, arithmetic and copies ran while one was open for 20% of the time, Pallas kernels for 0%

commit v1 on v0

v1 whole, which is shorter than its diff:
```python
import functools

import jax
import jax.numpy as jnp
from jax import lax
from jax.experimental import pallas as pl
from jax.experimental.pallas import tpu as pltpu
from jax.sharding import Mesh, PartitionSpec as P

DH = 128
CAP = 6
MESH = pl.DeviceIdType.MESH
F32 = jnp.float32
BF16 = jnp.bfloat16

cosine_divisor = 0.05
epsilon_norm = 1e-05
epsilon_unit = 1e-06

VM = pl.BlockSpec(memory_space=pltpu.VMEM)
SM = pl.BlockSpec(memory_space=pltpu.SMEM)


def sds(shape, dtype):
    return jax.ShapeDtypeStruct(shape, dtype)


def params(**kw):
    return pltpu.CompilerParams(vmem_limit_bytes=60 * 1024 * 1024, **kw)


def mp_id(m):
    return (lax.axis_index("x"), lax.axis_index("z"), lax.axis_index("c"), m)


def enter(peers):
    barrier = pltpu.get_barrier_semaphore()
    for peer in peers:
        pl.semaphore_signal(barrier, inc=1, device_id=peer, device_id_type=MESH)
    pl.semaphore_wait(barrier, len(peers))


def slots_kernel(own_ref, row_ref, want_ref, event_ref, rank_ref, col_ref):
    owners_n, events = rank_ref.shape
    who = lax.broadcasted_iota(jnp.int32, (owners_n, events), 0)
    named = jnp.zeros((owners_n, events), F32)
    rows = jnp.zeros((owners_n, events), jnp.int32)
    cols = jnp.zeros((owners_n, events), jnp.int32)
    for j in range(own_ref.shape[0]):
        mask = own_ref[j : j + 1, :] == who
        named = jnp.where(mask, 1.0, named)
        rows = jnp.where(mask, row_ref[j : j + 1, :], rows)
        cols = jnp.where(mask, j, cols)
    before = (
        lax.broadcasted_iota(jnp.int32, (events, events), 0)
        < lax.broadcasted_iota(jnp.int32, (events, events), 1)
    ).astype(F32)
    rank = jnp.dot(
        named.astype(BF16), before.astype(BF16), preferred_element_type=F32
    ).astype(jnp.int32)
    rank = jnp.where(named > 0.0, rank, -1)
    rank_ref[...] = rank
    col_ref[...] = cols
    event = lax.broadcasted_iota(jnp.int32, (owners_n, events), 1)
    lane = lax.broadcasted_iota(jnp.int32, want_ref.shape, 1)
    want = jnp.full(want_ref.shape, -1, jnp.int32)
    chosen = jnp.zeros(want_ref.shape, jnp.int32)
    for r in range(CAP):
        here = rank == r
        row_r = jnp.max(jnp.where(here, rows, -1), axis=1, keepdims=True)
        event_r = jnp.max(jnp.where(here, event, 0), axis=1, keepdims=True)
        want = jnp.where(lane == r, row_r, want)
        chosen = jnp.where(lane == r, event_r, chosen)
    want_ref[...] = want
    event_ref[...] = chosen


def slots(owners_t, rows_t, dev_count):
    events = owners_t.shape[1]
    table = sds((dev_count, 128), jnp.int32)
    wide = sds((dev_count, events), jnp.int32)
    return pl.pallas_call(
        slots_kernel,
        out_shape=(table, table, wide, wide),
        in_specs=[VM] * 2,
        out_specs=(VM,) * 4,
        compiler_params=params(),
        name="slots",
    )(owners_t, rows_t)


def gather_kernel(idx_ref, table_ref, out_ref):
    def one(s, carry):
        for r in range(CAP):
            out_ref[s, r] = table_ref[jnp.maximum(idx_ref[s, r], 0)]
        return carry

    lax.fori_loop(0, out_ref.shape[0], one, 0, unroll=4)


def gather_rows(idx, table):
    n = idx.shape[0]
    return pl.pallas_call(
        gather_kernel,
        out_shape=sds((n, CAP) + table.shape[1:], table.dtype),
        in_specs=[SM, VM],
        out_specs=VM,
        compiler_params=params(),
        name="gather_rows",
    )(idx, table)


def pick_kernel(idx_ref, table_ref, out_ref):
    def one(s, carry):
        out_ref[s] = table_ref[idx_ref[s]]
        return carry

    lax.fori_loop(0, out_ref.shape[0], one, 0, unroll=4)


def pick_blocks(idx, table):
    n = idx.shape[0]
    return pl.pallas_call(
        pick_kernel,
        out_shape=sds((n,) + table.shape[1:], table.dtype),
        in_specs=[SM, VM],
        out_specs=VM,
        compiler_params=params(),
        name="pick_blocks",
    )(idx, table)


def loss_kernel(
    items_ref, out_ref, rank_ref, col_ref, valid_ref, grad_ref, coef_ref, flat, mat, cosine, expo
):
    n, _, lanes_hi, lanes = items_ref.shape
    out = out_ref[...]
    inv_out = 1.0 / jnp.sqrt(jnp.sum(out * out, axis=-1, keepdims=True) + epsilon_unit)
    unit = out * inv_out
    unit_b = unit.astype(BF16)
    rank = rank_ref[...]
    total = jnp.zeros((1, rank.shape[1]), F32)
    inverse = []
    for r in range(CAP):
        flat[...] = items_ref[:, r].astype(F32).reshape(n * lanes_hi, lanes)
        squares = jnp.zeros((n, lanes), F32)
        for c in range(lanes_hi):
            chunk = flat[pl.ds(c, n, stride=lanes_hi), :]
            squares = squares + chunk * chunk
            mat[r, :, c * lanes : (c + 1) * lanes] = chunk.astype(BF16)
        inv = 1.0 / jnp.sqrt(jnp.sum(squares, axis=-1, keepdims=True) + epsilon_unit)
        inverse.append(inv)
        dots = lax.dot_general(
            mat[r], unit_b, (((1,), (1,)), ((), ())), preferred_element_type=F32
        )
        cos = dots * inv
        ex = jnp.where(rank == r, jnp.exp(cos / cosine_divisor), 0.0)
        cosine[r] = cos
        expo[r] = ex
        total = total + jnp.sum(ex, axis=0, keepdims=True)
    valid = valid_ref[0:1, :]
    scale = valid / total
    first = (col_ref[...] == 0).astype(F32) * valid
    lane = lax.broadcasted_iota(jnp.int32, coef_ref.shape, 1)
    coef = jnp.zeros(coef_ref.shape, F32)
    slope = jnp.zeros(out.shape, F32)
    for r in range(CAP):
        share = expo[r] * scale - jnp.where(rank == r, first, 0.0)
        weight = share * (inverse[r] / cosine_divisor)
        slope = slope + lax.dot_general(
            weight.astype(BF16), mat[r], (((0,), (0,)), ((), ())), preferred_element_type=F32
        )
        a = jnp.sum(weight, axis=-1, keepdims=True)
        b = jnp.sum(weight * cosine[r], axis=-1, keepdims=True) * inverse[r]
        coef = jnp.where(lane == r, a, coef)
        coef = jnp.where(lane == r + 8, b, coef)
    coef_ref[...] = coef
    along = jnp.sum(unit * slope, axis=-1, keepdims=True)
    grad_ref[...] = ((slope - unit * along) * inv_out).astype(BF16)


def loss_call(items, out_rows, rank, col, valid):
    n = items.shape[0]
    events, width = out_rows.shape
    return pl.pallas_call(
        loss_kernel,
        out_shape=(sds((events, width), BF16), sds((n, 128), F32)),
        in_specs=[VM] * 5,
        out_specs=(VM,) * 2,
        scratch_shapes=[
            pltpu.VMEM((n * items.shape[2], items.shape[3]), F32),
            pltpu.VMEM((CAP, n, width), BF16),
            pltpu.VMEM((CAP, n, events), F32),
            pltpu.VMEM((CAP, n, events), F32),
        ],
        compiler_params=params(),
        name="loss",
    )(items, out_rows, rank, col, valid)


def catalogue_kernel(units_ref, want_ref, coef_ref, cat_ref, out_ref, flat, mat, hot, side):
    n, _, lanes_hi, lanes = units_ref.shape
    rows = cat_ref.shape[0]
    want = want_ref[...]
    coef = coef_ref[...]
    row = lax.broadcasted_iota(jnp.int32, (n, rows), 1)
    lane = lax.broadcasted_iota(jnp.int32, (n, lanes), 1)
    for r in range(CAP):
        flat[...] = units_ref[:, r].astype(F32).reshape(n * lanes_hi, lanes)
        a = coef[:, r : r + 1]
        b = coef[:, r + 8 : r + 9]
        high = b.astype(BF16).astype(F32)
        span = pl.ds(r * n, n)
        for c in range(lanes_hi):
            chunk = flat[pl.ds(c, n, stride=lanes_hi), :]
            mat[span, c * lanes : (c + 1) * lanes] = (chunk * a).astype(BF16)
        side[span, :] = jnp.where(
            lane == 0, high, jnp.where(lane == 1, b - high, 0.0)
        ).astype(BF16)
        hot[span, :] = (want[:, r : r + 1] == row).astype(F32).astype(BF16)
    over = (((0,), (0,)), ((), ()))
    both = lax.dot_general(hot[...], side[...], over, preferred_element_type=F32)
    b_row = both[:, 0:1] + both[:, 1:2]
    for c in range(0, cat_ref.shape[1], 256):
        part = lax.dot_general(hot[...], mat[:, c : c + 256], over, preferred_element_type=F32)
        out_ref[:, c : c + 256] = part - b_row * cat_ref[:, c : c + 256].astype(F32)


def catalogue_call(units, want, coef, catalogue):
    n = units.shape[0]
    rows, width = catalogue.shape
    return pl.pallas_call(
        catalogue_kernel,
        out_shape=sds((rows, width), F32),
        in_specs=[VM] * 4,
        out_specs=VM,
        scratch_shapes=[
            pltpu.VMEM((n * units.shape[2], units.shape[3]), F32),
            pltpu.VMEM((CAP * n, width), BF16),
            pltpu.VMEM((CAP * n, rows), BF16),
            pltpu.VMEM((CAP * n, 128), BF16),
        ],
        compiler_params=params(),
        name="catalogue_grad",
    )(units, want, coef, catalogue)


def gather_mp_kernel(n, by_column, x_ref, out_ref, send, recv, local):
    me = lax.axis_index("mp")
    peers = [lax.rem(me + k, n) for k in range(1, n)]
    enter([mp_id(p) for p in peers])
    rows, cols = x_ref.shape
    if by_column:
        mine = out_ref.at[:, pl.ds(pl.multiple_of(me * cols, cols), cols)]
    else:
        mine = out_ref.at[pl.ds(pl.multiple_of(me * rows, rows), rows), :]
    copies = [
        pltpu.make_async_remote_copy(
            src_ref=x_ref,
            dst_ref=mine,
            send_sem=send.at[i],
            recv_sem=recv.at[i],
            device_id=mp_id(p),
            device_id_type=MESH,
        )
        for i, p in enumerate(peers)
    ]
    for copy in copies:
        copy.start()
    own = pltpu.make_async_copy(x_ref, mine, local)
    own.start()
    own.wait()
    for copy in copies:
        copy.wait()


def gather_mp(x, n, by_column, cid):
    rows, cols = x.shape
    shape = (rows, cols * n) if by_column else (rows * n, cols)
    return pl.pallas_call(
        functools.partial(gather_mp_kernel, n, by_column),
        out_shape=sds(shape, x.dtype),
        in_specs=[VM],
        out_specs=VM,
        scratch_shapes=[
            pltpu.SemaphoreType.DMA((n - 1,)),
            pltpu.SemaphoreType.DMA((n - 1,)),
            pltpu.SemaphoreType.DMA,
        ],
        compiler_params=params(collective_id=cid, has_side_effects=True),
        name="gather_mp",
    )(x)


def scatter_mp_kernel(n, gated_ref, w_ref, feat_ref, out_ref, unit_ref, staged, landed, send, recv):
    me = lax.axis_index("mp")
    peers = [lax.rem(me + k, n) for k in range(1, n)]
    quarter = out_ref.shape[0]

    def block(m):
        rows = pl.ds(pl.multiple_of(m * quarter, quarter), quarter)
        return jnp.dot(gated_ref[rows, :], w_ref[...], preferred_element_type=F32)

    enter([mp_id(p) for p in peers])
    for i, p in enumerate(peers):
        staged[i] = block(p).astype(BF16)
    copies = [
        pltpu.make_async_remote_copy(
            src_ref=staged.at[i],
            dst_ref=landed.at[i],
            send_sem=send.at[i],
            recv_sem=recv.at[i],
            device_id=mp_id(p),
            device_id_type=MESH,
        )
        for i, p in enumerate(peers)
    ]
    for copy in copies:
        copy.start()
    mine = pl.ds(pl.multiple_of(me * quarter, quarter), quarter)
    total = block(me) + feat_ref[mine, :].astype(F32)
    for i, copy in enumerate(copies):
        copy.wait()
        total = total + landed[i].astype(F32)
    out_ref[...] = total
    inv = 1.0 / jnp.sqrt(jnp.sum(total * total, axis=-1, keepdims=True) + epsilon_unit)
    unit_ref[...] = (total * inv).astype(BF16)


def scatter_mp(gated, w_out, features, n, cid):
    rows, width = features.shape
    quarter = rows // n
    return pl.pallas_call(
        functools.partial(scatter_mp_kernel, n),
        out_shape=(sds((quarter, width), F32), sds((quarter, width), BF16)),
        in_specs=[VM] * 3,
        out_specs=(VM,) * 2,
        scratch_shapes=[
            pltpu.VMEM((n - 1, quarter, width), BF16),
            pltpu.VMEM((n - 1, quarter, width), BF16),
            pltpu.SemaphoreType.DMA((n - 1,)),
            pltpu.SemaphoreType.DMA((n - 1,)),
        ],
        compiler_params=params(collective_id=cid, has_side_effects=True),
        name="scatter_mp",
    )(gated, w_out, features)


def weights_kernel(
    nx, nz, x_ref, out_ref, stage_x, stage_z, land_c, land_x, land_z,
    send_c, recv_c, send_x, recv_x, send_z, recv_z,
):
    ix, iz, ic, im = (lax.axis_index(a) for a in ("x", "z", "c", "mp"))
    peer_c = (ix, iz, 1 - ic, im)
    xs = [lax.rem(ix + k, nx) for k in range(1, nx)]
    zs = [lax.rem(iz + k, nz) for k in range(1, nz)]
    peers_x = [(p, iz, ic, im) for p in xs]
    peers_z = [(ix, p, ic, im) for p in zs]
    enter([peer_c] + peers_x + peers_z)
    first = pltpu.make_async_remote_copy(
        src_ref=x_ref.at[:, :, :, 1 - ic],
        dst_ref=land_c,
        send_sem=send_c,
        recv_sem=recv_c,
        device_id=peer_c,
        device_id_type=MESH,
    )
    first.start()
    first.wait()
    copies = []
    for i, p in enumerate(xs):
        stage_x[i] = (x_ref[:, p, :, ic].astype(F32) + land_c[:, p].astype(F32)).astype(BF16)
        copies.append(
            pltpu.make_async_remote_copy(
                src_ref=stage_x.at[i],
                dst_ref=land_x.at[i],
                send_sem=send_x.at[i],
                recv_sem=recv_x.at[i],
                device_id=peers_x[i],
                device_id_type=MESH,
            )
        )
        copies[-1].start()
    total = x_ref[:, ix, :, ic].astype(F32) + land_c[:, ix].astype(F32)
    for i, copy in enumerate(copies):
        copy.wait()
        total = total + land_x[i].astype(F32)
    stage_z[...] = total.astype(BF16)
    copies = []
    for i, p in enumerate(zs):
        copies.append(
            pltpu.make_async_remote_copy(
                src_ref=stage_z.at[:, p],
                dst_ref=land_z.at[i],
                send_sem=send_z.at[i],
                recv_sem=recv_z.at[i],
                device_id=peers_z[i],
                device_id_type=MESH,
            )
        )
        copies[-1].start()
    result = stage_z[:, iz].astype(F32)
    for i, copy in enumerate(copies):
        copy.wait()
        result = result + land_z[i].astype(F32)
    out_ref[...] = result


def reduce_weights(parts, cid):
    groups, nx, nz, nc, rows, cols = parts.shape
    dma = pltpu.SemaphoreType.DMA
    return pl.pallas_call(
        functools.partial(weights_kernel, nx, nz),
        out_shape=sds((groups, rows, cols), F32),
        in_specs=[VM],
        out_specs=VM,
        scratch_shapes=[
            pltpu.VMEM((nx - 1, groups, nz, rows, cols), BF16),
            pltpu.VMEM((groups, nz, rows, cols), BF16),
            pltpu.VMEM((groups, nx, nz, rows, cols), BF16),
            pltpu.VMEM((nx - 1, groups, nz, rows, cols), BF16),
            pltpu.VMEM((nz - 1, groups, rows, cols), BF16),
            dma, dma, dma((nx - 1,)), dma((nx - 1,)), dma((nz - 1,)), dma((nz - 1,)),
        ],
        compiler_params=params(collective_id=cid, has_side_effects=True),
        name="reduce_weights",
    )(parts)


def normalize(rows_in):
    centered = rows_in - jnp.mean(rows_in, axis=-1, keepdims=True)
    spread = jnp.mean(centered * centered, axis=-1, keepdims=True)
    return centered / jnp.sqrt(spread + epsilon_norm)


def attend(projected, length_here):
    gating = projected[0]
    values = projected[1]
    queries = projected[2]
    key_rows = projected[3]
    steps_n = projected.shape[1]
    scores = jnp.einsum(
        "thd,shd->hts", queries, key_rows, preferred_element_type=jnp.float32
    ) / jnp.sqrt(jnp.float32(projected.shape[3]))
    places = jnp.arange(steps_n, dtype=jnp.int32)
    allowed = (places[None, :] <= places[:, None]) & (places[None, :] < length_here)
    weights = jnp.where(
        allowed[None], jax.nn.silu(scores) / length_here.astype(jnp.float32), 0.0
    ).astype(jnp.bfloat16)
    mixed_out = jnp.einsum("hts,shd->thd", weights, values, preferred_element_type=jnp.float32)
    return (normalize(mixed_out) * gating.astype(jnp.float32)).astype(jnp.bfloat16)


def silu_slope(preact):
    sigma = jax.nn.sigmoid(preact)
    return sigma * (1.0 + preact * (1.0 - sigma))


ALL = ("x", "z", "c", "mp")
DP = ("x", "z", "c")


def exchange(x, axes):
    return lax.all_to_all(x, axes, split_axis=0, concat_axis=0, tiled=True)


def per_device(history, lengths, source, owners, item_rows, catalogue, w_in, w_out):
    nx, nz, nc, mp_count = (lax.axis_size(a) for a in ALL)
    dp_count = nx * nz * nc
    dev_count = dp_count * mp_count
    here_dp = (lax.axis_index("x") * nz + lax.axis_index("z")) * nc + lax.axis_index("c")
    here_mp = lax.axis_index("mp")
    seq_dev, steps_n, cols_here = history.shape
    seq_total = source.shape[0]
    rows_all = seq_dev * steps_n
    quarter = rows_all // mp_count
    width = catalogue.shape[1]

    want, chosen, rank, col = slots(owners.T, item_rows.T, dev_count)
    asked = exchange(want.reshape(dev_count, 1, 128), ALL).reshape(dev_count, 128)

    slot_ids = jnp.arange(seq_dev, dtype=jnp.int32)
    my_seqs = here_dp * seq_dev + slot_ids
    places = jnp.arange(seq_total, dtype=jnp.int32)
    target = jnp.sum(jnp.where(source[None, :] == my_seqs[:, None], places[None, :], 0), axis=1)
    dest_dev = target // seq_dev
    dests = jnp.arange(dp_count, dtype=jnp.int32)
    seq_for = jnp.sum(jnp.where(dest_dev[None, :] == dests[:, None], slot_ids[None, :], 0), axis=1)
    taken = lax.dynamic_slice_in_dim(source, here_dp * seq_dev, seq_dev, 0)
    counts = jnp.sum(jnp.where(places[None, :] == taken[:, None], lengths[None, :], 0), axis=1)
    arrived = exchange(pick_blocks(seq_for, history), DP)
    local_rows = pick_blocks(taken // seq_dev, arrived).reshape(rows_all, cols_here)

    tiles = catalogue.reshape(catalogue.shape[0], width // 128, 128)
    fetched = exchange(gather_rows(asked, tiles), ALL)

    flat_rows = gather_mp(local_rows, mp_count, True, 1)
    normed = normalize(flat_rows.astype(jnp.float32)).astype(jnp.bfloat16)
    preact = jnp.einsum("rd,cdh->crh", normed, w_in, preferred_element_type=jnp.float32)
    projected = jax.nn.silu(preact).astype(jnp.bfloat16)
    cols_heads = w_in.shape[2]
    heads_here = cols_heads // DH
    grouped = projected.reshape(4, seq_dev, steps_n, heads_here, DH)

    def run_all(inputs):
        return jax.vmap(attend, in_axes=(1, 0))(inputs, counts)

    gated, back = jax.vjp(run_all, grouped)
    gated_flat = gated.reshape(rows_all, cols_heads)
    out_rows, unit_rows = scatter_mp(gated_flat, w_out, flat_rows, mp_count, 2)
    unit_tiles = unit_rows.reshape(quarter, width // 128, 128)
    units = gather_rows(chosen, unit_tiles)
    fetched, units = lax.optimization_barrier((fetched, units))
    landed = exchange(units, ALL)

    position = here_mp * quarter + jnp.arange(quarter, dtype=jnp.int32)
    count_of = jnp.sum(
        jnp.where((position // steps_n)[:, None] == slot_ids[None, :], counts[None, :], 0), axis=1
    )
    valid = jnp.broadcast_to((position % steps_n < count_of).astype(F32)[None, :], (8, quarter))
    out_grad, coef = loss_call(fetched, out_rows, rank, col, valid)
    coefs = exchange(coef.reshape(dev_count, 1, 128), ALL).reshape(dev_count, 128)

    out_cotangent = gather_mp(out_grad, mp_count, False, 3)
    w_out_part = jnp.einsum(
        "rd,rh->dh", out_cotangent, gated_flat, preferred_element_type=jnp.float32
    )
    gated_cotangent = jnp.einsum(
        "rd,hd->rh", out_cotangent, w_out, preferred_element_type=jnp.float32
    ).astype(jnp.bfloat16)
    (grouped_cotangent,) = back(gated_cotangent.reshape(seq_dev, steps_n, heads_here, DH))
    projected_cotangent = grouped_cotangent.reshape(4, rows_all, cols_heads)
    preact_cotangent = (projected_cotangent.astype(jnp.float32) * silu_slope(preact)).astype(
        jnp.bfloat16
    )
    w_in_part = jnp.einsum(
        "rd,crh->cdh", normed, preact_cotangent, preferred_element_type=jnp.float32
    )
    parts = jnp.concatenate([w_in_part.astype(BF16), w_out_part.astype(BF16)[None]], axis=0)
    rows_out = width // dp_count
    sums = reduce_weights(parts.reshape(5, nx, nz, nc, rows_out, cols_heads), 4)
    cat_grad = catalogue_call(landed, asked, coefs, catalogue)
    return (sums[:4], sums[4].T, cat_grad)


def solution(mesh):
    split = Mesh(mesh.devices.reshape(4, 8, 2, 4), ALL)
    placed = (
        P(DP, None, "mp"),
        P(),
        P(),
        P(ALL, None),
        P(ALL, None),
        P(ALL, None),
        P(None, None, "mp"),
        P("mp", None),
    )
    return jax.shard_map(
        per_device,
        mesh=split,
        in_specs=placed,
        out_specs=(P(None, DP, "mp"), P("mp", DP), P(ALL, None)),
        check_vma=False,
    )
```

time: 695 us -> 306 us (0.44); the launches traced: 684 us -> 304 us
  waiting for transfers between devices: 419 us -> 29.1 us
  Pallas kernels: 0 us -> 158 us
  local copies, waits for them, and re-layouts: 123 us -> 25 us
  other arithmetic: 55.5 us -> 12.6 us
  blocking collectives: 0 us -> 26.8 us
  between operations: 16 us -> 0.99 us
  starting transfers between devices: 47.7 us -> 37 us
    unnamed x6 -> x0, waiting for transfers between devices: 161 us -> none
    pallas_call x0 -> x11, Pallas kernels: none -> 158 us  [the longest x2 55.9 us: gather_mp(): pl.pallas_call(functools.partial(gather_mp_kernel, n, by_column), out_sha...]
    reduce_scatter x1 -> x0, waiting for transfers between devices: 109 us -> none  [per_device(): lax.psum_scatter(w_out_part, 'dp', scatter_dimension=1, tiled=True)]
    all_gather x2 -> x0, waiting for transfers between devices: 53.8 us -> none  [the longest x1 28.8 us: per_device(): lax.all_gather(out_grad.astype(jnp.bfloat16), 'mp', axis=0, tiled=True)]
    gather x13 -> x0, local copies, waits for them, and re-layouts: 42.3 us -> none  [the longest x2 12.1 us: per_device(): jnp.take(catalogue, incoming_flat, axis=0)]
    all_to_all x7 -> x4, waiting for transfers between devices: 69.5 us -> 29.1 us  [exchange(): return lax.all_to_all(x, axes, split_axis=0, concat_axis=0, tiled=True)]
    all_to_all x0 -> x1, blocking collectives: none -> 26.8 us  [exchange(): return lax.all_to_all(x, axes, split_axis=0, concat_axis=0, tiled=True)]
    psum x1 -> x0, waiting for transfers between devices: 25.9 us -> none  [per_device(): summed = lax.psum(partial_out, 'mp')]
  transfers between devices with their start and end apart: 12 -> 4, of which waited for: 11 -> 2; matrix products, arithmetic and copies ran while one was open for 20% -> 16% of each run, Pallas kernels for 0% -> 46%
where the time goes in v1:
time: 306 us; the launch traced here: 304 us
  Pallas kernels  158 us (52%)
  starting transfers between devices  37 us (12%)
  waiting for transfers between devices  29.1 us (10%)
  blocking collectives  26.8 us (9%)
  local copies, waits for them, and re-layouts  25 us (8%)
  matrix products  15.3 us (5%)
  other arithmetic  12.6 us (4%)
    pallas_call x2, Pallas kernels, gather_mp(): pl.pallas_call(functools.partial(gather_mp_kernel, n, by_column), out_sha...  55.9 us
    pallas_call x1, Pallas kernels, reduce_weights(): pl.pallas_call(functools.partial(weights_kernel, nx, nz), out_shape=sds((...  39.5 us
    all_to_all x4, starting transfers between devices, exchange(): return lax.all_to_all(x, axes, split_axis=0, concat_axis=0, tiled=True)  37 us
    all_to_all x4, waiting for transfers between devices, exchange(): return lax.all_to_all(x, axes, split_axis=0, concat_axis=0, tiled=True)  29.1 us
    all_to_all x1, blocking collectives, exchange(): return lax.all_to_all(x, axes, split_axis=0, concat_axis=0, tiled=True)  26.8 us
    pallas_call x1, Pallas kernels, scatter_mp(): pl.pallas_call(functools.partial(scatter_mp_kernel, n), out_shape=(sds((q...  26.3 us
    pallas_call x2, Pallas kernels, gather_rows(): pl.pallas_call(gather_kernel, out_shape=sds((n, CAP) + table.shape[1:], t...  14.4 us
    pallas_call x1, Pallas kernels, catalogue_call(): pl.pallas_call(catalogue_kernel, out_shape=sds((rows, width), F32), in_sp...  7.62 us
  transfers between devices with their start and end apart: 4, of which 2 were waited for; matrix products, arithmetic and copies ran while one was open for 16% of the time, Pallas kernels for 46%

profile of v1, /device:TPU:1, one launch (start us, length us, event | category | flops | bytes accessed | tf_op | source)
XLA Modules:
  0.0 304.4 jit_solution(12424852082712121607)
XLA Ops:
  0.7 3.0 slots.1
  3.6 15.6 %all-to-all-start = ((s32[256,1,128]{2,1,0:T(1,128)}), s32[256,1,128]{2,1,0:T(1,128)S(1)}, u32[]{:S(2)}, u32[]{:S(2)}) async-start(s32[256,1,128]{2,1,0:T(1,128)} %bitcast.104), calls=%async_computation | async-start | bytes 262144 | tf_op jit(solution)/shard_map/all_to_all | solution.py:464
  20.8 2.1 pick_blocks.2
  22.9 9.1 %all-to-all-done = s32[256,1,128]{2,1,0:T(1,128)S(1)} async-done(((s32[256,1,128]{2,1,0:T(1,128)}), s32[256,1,128]{2,1,0:T(1,128)S(1)}, u32[]{:S(2)}, u32[]{:S(2)}) %all-to-all-start) | async-done | bytes 131104 | tf_op jit(solution)/shard_map/all_to_all | solution.py:464
  32.0 5.8 %all-to-all-start.2 = ((bf16[64,32,256]{2,1,0:T(8,128)(2,1)}), bf16[64,32,256]{2,1,0:T(8,128)(2,1)}, u32[]{:S(2)}, u32[]{:S(2)}) async-start(bf16[64,32,256]{2,1,0:T(8,128)(2,1)} %pick_blocks.2), calls=%async_computation.2 | async-start | bytes 2097152 | tf_op jit(solution)/shard_map/all_to_all | solution.py:464
  39.1 7.2 %gather_rows.2 = bf16[256,6,8,128]{3,2,1,0:T(8,128)(2,1)} custom-call(s32[256,128]{1,0:T(8,128)} %bitcast.94, bf16[512,8,128]{2,1,0:T(8,128)(2,1)} %bitcast.93), custom_call_target="tpu_custom_call" | custom-call | tf_op jit(solution)/shard_map/gather_rows/pallas_call | solution.py:103
  46.3 20.0 %all-to-all-done.2.table_ref = bf16[64,32,256]{2,1,0:T(8,128)(2,1)} async-done(((bf16[64,32,256]{2,1,0:T(8,128)(2,1)}), bf16[64,32,256]{2,1,0:T(8,128)(2,1)}, u32[]{:S(2)}, u32[]{:S(2)}) %all-to-all-start.2) | async-done | bytes 1048608 | tf_op jit(solution)/shard_map/all_to_all | solution.py:464
  66.3 7.5 %all-to-all-start.1 = ((bf16[256,6,8,128]{3,2,1,0:T(8,128)(2,1)}), bf16[256,6,8,128]{3,2,1,0:T(8,128)(2,1)}, u32[]{:S(2)}, u32[]{:S(2)}) async-start(bf16[256,6,8,128]{3,2,1,0:T(8,128)(2,1)} %gather_rows.2), calls=%async_computation.1 | async-start | bytes 6291456 | tf_op jit(solution)/shard_map/all_to_all | solution.py:464
  75.5 2.0 pick_blocks.3
  77.5 26.3 %gather_mp.2.feat_ref = bf16[512,1024]{1,0:T(8,128)(2,1)} custom-call(bf16[512,256]{1,0:T(8,128)(2,1)} %bitcast.96), custom_call_target="tpu_custom_call" | custom-call | tf_op jit(solution)/shard_map/gather_mp/pallas_call | solution.py:280
  103.8 1.5 convert_reduce_fusion
  105.3 1.6 fusion.2
  107.0 2.8 fusion.7
  111.8 2.1 select_convert_fusion
  116.9 26.3 %scatter_mp.1 = (f32[128,1024]{1,0:T(8,128)}, bf16[128,1024]{1,0:T(8,128)(2,1)}) custom-call(bf16[512,256]{1,0:T(8,128)(2,1)} %bitcast.97, bf16[256,1024]{1,0:T(8,128)(2,1)} %w_ref.1, bf16[512,1024]{1,0:T(8,128)(2,1)} %gather_mp.2.feat_ref), custom_call_target="tpu_custom_call" | custom-call | tf_op jit(solution)/shard_map/scatter_mp/pallas_call | solution.py:333
  143.2 1.7 copy.82
  144.9 7.2 %gather_rows.3 = bf16[256,6,8,128]{3,2,1,0:T(8,128)(2,1)} custom-call(s32[256,128]{1,0:T(8,128)} %get-tuple-element.14.idx_ref, bf16[128,8,128]{2,1,0:T(8,128)(2,1)} %bitcast.98), custom_call_target="tpu_custom_call" | custom-call | tf_op jit(solution)/shard_map/gather_rows/pallas_call | solution.py:103
  152.7 7.0 %loss.1 = (bf16[128,1024]{1,0:T(8,128)(2,1)}, f32[256,128]{1,0:T(8,128)}) custom-call(bf16[256,6,8,128]{3,2,1,0:T(8,128)(2,1)} %all-to-all-done.1.items_ref, f32[128,1024]{1,0:T(8,128)} %get-tuple-element.17.out_ref, s32[256,128]{1,0:T(8,128)} %get-tuple-element.18.rank_ref, s32[256,128]{1,0:T(8,128)} %get-tuple-element.19.col_ref, ...), custom_call_target="tpu_custom_call" | custom-call | tf_op jit(solution)/shard_map/loss/pallas_call | solution.py:185
  159.6 26.8 %all_to_all.25 = f32[256,1,128]{2,1,0:T(1,128)} all-to-all(f32[256,1,128]{2,1,0:T(1,128)} %bitcast.105), channel_id=1, replica_groups=mesh['x'=4,'z'=8,'c'=2,'mp'=4] {'x','z','c','mp'}, dimensions={0} | all-to-all | bytes 262144 | tf_op jit(solution)/shard_map/all_to_all | solution.py:464
  186.4 8.0 %all-to-all-start.3 = ((bf16[256,6,8,128]{3,2,1,0:T(8,128)(2,1)}), bf16[256,6,8,128]{3,2,1,0:T(8,128)(2,1)}, u32[]{:S(2)}, u32[]{:S(2)}) async-start(bf16[256,6,8,128]{3,2,1,0:T(8,128)(2,1)} %gather_rows.3), calls=%async_computation.3 | async-start | bytes 6291456 | tf_op jit(solution)/shard_map/all_to_all | solution.py:464
  194.4 29.7 %gather_mp.3 = bf16[512,1024]{1,0:T(8,128)(2,1)} custom-call(bf16[128,1024]{1,0:T(8,128)(2,1)} %get-tuple-element.20.x_ref), custom_call_target="tpu_custom_call" | custom-call | tf_op jit(solution)/shard_map/gather_mp/pallas_call | solution.py:280
  224.1 2.6 fusion.15
  226.7 2.1 reshape.202
  228.8 1.6 multiply_reduce_fusion
  230.5 1.7 fusion.44
  234.3 3.2 %copy.73 = f32[4,16,32,2,128]{4,3,2,1,0:T(2,128)} copy(f32[4,16,32,2,128]{4,2,3,1,0:T(8,128)S(1)} %add_convert_fusion) | data formatting | bytes 4194304 | tf_op jit(solution)/shard_map/convert_element_type | solution.py:533
  237.6 4.0 %reshape.203 = f32[4,512,256]{2,1,0:T(8,128)} reshape(f32[4,16,32,2,128]{4,3,2,1,0:T(2,128)} %copy.73) | data formatting | bytes 4194304 | tf_op jit(solution)/shard_map/convert_element_type | solution.py:533
  241.6 5.5 %convert_bitcast_fusion = bf16[4,1024,256]{1,2,0:T(8,128)(2,1)} fusion(f32[4,512,256]{2,1,0:T(8,128)} %reshape.203, f32[512,4,256]{2,0,1:T(8,128)} %get-tuple-element.35, bf16[512,1024]{1,0:T(8,128)(2,1)S(1)} %copy-done.2, f32[512]{0:T(512)S(1)} %add_sqrt_fusion, f32[512]{0:T(512)S(1)} %broadcast_multiply_fusion.1), kind=kOutput, calls=%fused_computation.18 | convolution fusion | flops 1081606144 | bytes 7344128 | tf_op jit(solution)/shard_map/rd,crh->cdh/dot_general | solution.py:536
  247.1 4.0 %copy.75 = bf16[4,1024,256]{2,1,0:T(8,128)(2,1)} copy(bf16[4,1024,256]{1,2,0:T(8,128)(2,1)} %convert_bitcast_fusion) | data formatting | bytes 4194304 | tf_op jit(solution)/shard_map/convert_element_type | solution.py:539
  252.7 1.8 pad_maximum_fusion.x_ref
  254.5 39.5 %reduce_weights.1 = f32[5,16,256]{2,1,0:T(8,128)} custom-call(bf16[5,4,8,2,16,256]{5,4,3,2,1,0:T(8,128)(2,1)} %pad_maximum_fusion.x_ref), custom_call_target="tpu_custom_call" | custom-call | tf_op jit(solution)/shard_map/reduce_weights/pallas_call | solution.py:412
  296.8 7.6 %catalogue_grad.1 = f32[512,1024]{1,0:T(8,128)} custom-call(bf16[256,6,8,128]{3,2,1,0:T(8,128)(2,1)} %all-to-all-done.3.units_ref, s32[256,128]{1,0:T(8,128)} %bitcast.95, f32[256,128]{1,0:T(8,128)} %bitcast.102, bf16[512,1024]{1,0:T(8,128)(2,1)} %cat_ref.1), custom_call_target="tpu_custom_call" | custom-call | tf_op jit(solution)/shard_map/catalogue_grad/pallas_call | solution.py:232
  (73 shorter events, 16.4 us)
Async XLA Ops:
  0.6 106.4 %copy-start = (bf16[4,1024,256]{2,1,0:T(8,128)(2,1)S(1)}, bf16[4,1024,256]{2,1,0:T(8,128)(2,1)}, u32[]{:S(2)}) copy-start(bf16[4,1024,256]{2,1,0:T(8,128)(2,1)} %param.14) | copy-start | bytes 6291460
  0.6 37.2 %copy-start.4 = (bf16[512,1024]{1,0:T(8,128)(2,1)S(1)}, bf16[512,1024]{1,0:T(8,128)(2,1)}, u32[]{:S(2)}) copy-start(bf16[512,1024]{1,0:T(8,128)(2,1)} %cat_ref.1) | copy-start | bytes 3145732
  3.6 28.4 %all-to-all-start = ((s32[256,1,128]{2,1,0:T(1,128)}), s32[256,1,128]{2,1,0:T(1,128)S(1)}, u32[]{:S(2)}, u32[]{:S(2)}) async-start(s32[256,1,128]{2,1,0:T(1,128)} %bitcast.104), calls=%async_computation | async-start | bytes 262144 | tf_op jit(solution)/shard_map/all_to_all | solution.py:464
  32.0 7.1 %copy-start.6 = (s32[256,1,128]{2,1,0:T(1,128)}, s32[256,1,128]{2,1,0:T(1,128)S(1)}, u32[]{:S(2)}) copy-start(s32[256,1,128]{2,1,0:T(1,128)S(1)} %all-to-all-done) | copy-start | bytes 393220
  32.0 34.3 %all-to-all-start.2 = ((bf16[64,32,256]{2,1,0:T(8,128)(2,1)}), bf16[64,32,256]{2,1,0:T(8,128)(2,1)}, u32[]{:S(2)}, u32[]{:S(2)}) async-start(bf16[64,32,256]{2,1,0:T(8,128)(2,1)} %pick_blocks.2), calls=%async_computation.2 | async-start | bytes 2097152 | tf_op jit(solution)/shard_map/all_to_all | solution.py:464
  46.3 28.8 %copy-start.14 = (s32[1024]{0:T(1024)S(1)}, s32[1024]{0:T(1024)}, u32[]{:S(2)}) copy-start(s32[1024]{0:T(1024)} %param.9) | copy-start | bytes 12292
  66.3 85.8 %all-to-all-start.1 = ((bf16[256,6,8,128]{3,2,1,0:T(8,128)(2,1)}), bf16[256,6,8,128]{3,2,1,0:T(8,128)(2,1)}, u32[]{:S(2)}, u32[]{:S(2)}) async-start(bf16[256,6,8,128]{3,2,1,0:T(8,128)(2,1)} %gather_rows.2), calls=%async_computation.1 | async-start | bytes 6291456 | tf_op jit(solution)/shard_map/all_to_all | solution.py:464
  103.8 3.2 %copy-start.1 = (bf16[512,1024]{1,0:T(8,128)(2,1)S(1)}, bf16[512,1024]{1,0:T(8,128)(2,1)}, u32[]{:S(2)}) copy-start(bf16[512,1024]{1,0:T(8,128)(2,1)} %gather_mp.2.feat_ref) | copy-start | bytes 3145732
  111.8 2.1 copy-start.10
  113.9 0.9 copy-start.12
  115.4 0.7 copy-start.8
  186.4 110.4 %all-to-all-start.3 = ((bf16[256,6,8,128]{3,2,1,0:T(8,128)(2,1)}), bf16[256,6,8,128]{3,2,1,0:T(8,128)(2,1)}, u32[]{:S(2)}, u32[]{:S(2)}) async-start(bf16[256,6,8,128]{3,2,1,0:T(8,128)(2,1)} %gather_rows.3), calls=%async_computation.3 | async-start | bytes 6291456 | tf_op jit(solution)/shard_map/all_to_all | solution.py:464
  228.8 3.4 %copy-start.11 = (bf16[16,32,2,128]{3,2,1,0:T(2,128)(2,1)S(1)}, bf16[16,32,2,128]{3,2,1,0:T(2,128)(2,1)}, u32[]{:S(2)}) copy-start(bf16[16,32,2,128]{3,2,1,0:T(2,128)(2,1)} %transpose.73) | copy-start | bytes 786436
  228.8 3.4 %copy-start.15 = (f32[16,2,32,32]{3,2,1,0:T(8,128)S(1)}, f32[16,2,32,32]{3,2,1,0:T(8,128)}, u32[]{:S(2)}) copy-start(f32[16,2,32,32]{3,2,1,0:T(8,128)} %get-tuple-element.37) | copy-start | bytes 393220
  232.2 1.0 copy-start.7
  232.2 1.4 copy-start.13
  237.6 4.0 %copy-start.2 = (bf16[512,1024]{1,0:T(8,128)(2,1)S(1)}, bf16[512,1024]{1,0:T(8,128)(2,1)}, u32[]{:S(2)}) copy-start(bf16[512,1024]{1,0:T(8,128)(2,1)} %gather_mp.2.feat_ref) | copy-start | bytes 3145732
  247.0 4.0 %copy-start.5 = (bf16[512,1024]{1,0:T(8,128)(2,1)S(1)}, bf16[512,1024]{1,0:T(8,128)(2,1)}, u32[]{:S(2)}) copy-start(bf16[512,1024]{1,0:T(8,128)(2,1)} %gather_mp.3) | copy-start | bytes 3145732
  247.0 4.0 %copy-start.9 = (bf16[16,32,2,128]{3,2,1,0:T(2,128)(2,1)S(1)}, bf16[16,32,2,128]{3,2,1,0:T(2,128)(2,1)}, u32[]{:S(2)}) copy-start(bf16[16,32,2,128]{3,2,1,0:T(2,128)(2,1)} %copy-done.8) | copy-start | bytes 786436
  251.1 1.6 copy-start.3

commit v2 on v0

v2 whole, which is shorter than its diff:
```python
import functools

import jax
import jax.numpy as jnp
from jax import lax
from jax.experimental import pallas as pl
from jax.experimental.pallas import tpu as pltpu
from jax.sharding import Mesh, PartitionSpec as P

DH = 128
CAP = 6
MESH = pl.DeviceIdType.MESH
F32 = jnp.float32
BF16 = jnp.bfloat16

cosine_divisor = 0.05
epsilon_norm = 1e-05
epsilon_unit = 1e-06

VM = pl.BlockSpec(memory_space=pltpu.VMEM)
SM = pl.BlockSpec(memory_space=pltpu.SMEM)


def sds(shape, dtype):
    return jax.ShapeDtypeStruct(shape, dtype)


def params(**kw):
    return pltpu.CompilerParams(vmem_limit_bytes=60 * 1024 * 1024, **kw)


def slots_kernel(own_ref, row_ref, want_ref, event_ref, rank_ref, col_ref):
    owners_n, events = rank_ref.shape
    who = lax.broadcasted_iota(jnp.int32, (owners_n, events), 0)
    named = jnp.zeros((owners_n, events), F32)
    rows = jnp.zeros((owners_n, events), jnp.int32)
    cols = jnp.zeros((owners_n, events), jnp.int32)
    for j in range(own_ref.shape[0]):
        mask = own_ref[j : j + 1, :] == who
        named = jnp.where(mask, 1.0, named)
        rows = jnp.where(mask, row_ref[j : j + 1, :], rows)
        cols = jnp.where(mask, j, cols)
    before = (
        lax.broadcasted_iota(jnp.int32, (events, events), 0)
        < lax.broadcasted_iota(jnp.int32, (events, events), 1)
    ).astype(F32)
    rank = jnp.dot(
        named.astype(BF16), before.astype(BF16), preferred_element_type=F32
    ).astype(jnp.int32)
    rank = jnp.where(named > 0.0, rank, -1)
    rank_ref[...] = rank
    col_ref[...] = cols
    event = lax.broadcasted_iota(jnp.int32, (owners_n, events), 1)
    lane = lax.broadcasted_iota(jnp.int32, want_ref.shape, 1)
    want = jnp.full(want_ref.shape, -1, jnp.int32)
    chosen = jnp.zeros(want_ref.shape, jnp.int32)
    for r in range(CAP):
        here = rank == r
        row_r = jnp.max(jnp.where(here, rows, -1), axis=1, keepdims=True)
        event_r = jnp.max(jnp.where(here, event, 0), axis=1, keepdims=True)
        want = jnp.where(lane == r, row_r, want)
        chosen = jnp.where(lane == r, event_r, chosen)
    want_ref[...] = want
    event_ref[...] = chosen


OVER_ROWS = (((0,), (0,)), ((), ()))
OVER_COLS = (((1,), (1,)), ((), ()))


def sigmoid(v):
    return 1.0 / (1.0 + jnp.exp(-v))


def silu_slope(v):
    s = sigmoid(v)
    return s * (1.0 + v * (1.0 - s))


def center(v):
    moved = v - jnp.mean(v, axis=-1, keepdims=True)
    inv = 1.0 / jnp.sqrt(jnp.mean(moved * moved, axis=-1, keepdims=True) + epsilon_norm)
    return moved * inv, inv


def attention_weights(q, k, count):
    n = q.shape[0]
    scores = lax.dot_general(q, k, OVER_COLS, preferred_element_type=F32) * (DH**-0.5)
    t = lax.broadcasted_iota(jnp.int32, (n, n), 0)
    s = lax.broadcasted_iota(jnp.int32, (n, n), 1)
    first = t - lax.rem(t, STEPS)
    mask = (s >= first) & (s <= t) & ((s - first).astype(F32) < count)
    return scores, mask


STEPS = 32


def step_kernel(
    seq_for, anchors, owners_ref, rows_ref, count_ref, valid_ref,
    history_hbm, tiles_hbm, cat_hbm, w_in_hbm, w_out_hbm,
    cat_grad_ref, sums_ref,
    hist, hist_out, arrived, tiles, cat, w_in, w_out, load_sem,
    want, event, rank, col, chosen_v, want_out, asked, asked_s, chosen_s, small_sem,
    fetch_out, fetch_in, unit_out, unit_in, coef_out, coef_in,
    part, flat, normed, preact, proj, gated, staged, landed,
    out_rows, tall, mat, cosine, expo, grad, cot, gated_cot, pre_cot,
    parts, land_c, stage_x, land_x, stage_z, land_z, hot, side,
    ids_sem, hist_sem, fetch_sem, unit_sem, coef_sem, gat_sem, sca_sem, cot_sem,
    c_sem, x_sem, z_sem,
):
    ix, iz, ic, im = (lax.axis_index(a) for a in ALL)
    nx, nz, nc, nm = NX, NZ, NC, NM
    n = nx * nz * nc * nm
    here_dp = (ix * nz + iz) * nc + ic
    me = here_dp * nm + im
    n_dp = nx * nz * nc

    def dp_at(d):
        return (lax.div(d, nz * nc), lax.rem(lax.div(d, nc), nz), lax.rem(d, nc))

    def device(d):
        return dp_at(lax.div(d, nm)) + (lax.rem(d, nm),)

    loads = [
        pltpu.make_async_copy(a, b, load_sem.at[i])
        for i, (a, b) in enumerate(
            [(history_hbm, hist), (tiles_hbm, tiles), (w_in_hbm, w_in), (w_out_hbm, w_out), (cat_hbm, cat)]
        )
    ]
    for load in loads:
        load.start()

    barrier = pltpu.get_barrier_semaphore()

    def greet(k, carry):
        pl.semaphore_signal(
            barrier, inc=1, device_id=device(lax.rem(me + k, n)), device_id_type=MESH
        )
        return carry

    lax.fori_loop(1, n, greet, 0)

    slots_kernel(owners_ref, rows_ref, want, event, rank, col)
    want_out[...] = want[...].reshape(want_out.shape)
    chosen_v[...] = event[...].reshape(chosen_v.shape)
    to_smem = pltpu.make_async_copy(chosen_v, chosen_s, small_sem.at[0])
    to_smem.start()
    loads[0].wait()

    def stage(d, carry):
        hist_out[d] = hist[seq_for[d]]
        return carry

    lax.fori_loop(0, n_dp, stage, 0, unroll=4)
    pl.semaphore_wait(barrier, n - 1)

    def send_all(src, dst, sems, first=1, last=n):
        def one(k, carry):
            d = lax.rem(me + k, n)
            push(src, dst, sems, d)
            return carry

        lax.fori_loop(first, last, one, 0)

    def push(src, dst, sems, d):
        pltpu.make_async_remote_copy(
            src_ref=src.at[d],
            dst_ref=dst.at[me],
            send_sem=sems.at[0],
            recv_sem=sems.at[1],
            device_id=device(d),
            device_id_type=MESH,
        ).start()

    def finish(ref, sems, which, count):
        block = ref.at[pl.ds(0, count)]
        pltpu.make_async_copy(block, block, sems.at[which]).wait()

    send_all(want_out, asked, ids_sem)
    asked[me] = want_out[me]

    def send_history(k, carry):
        d = lax.rem(here_dp + k, n_dp)
        pltpu.make_async_remote_copy(
            src_ref=hist_out.at[d],
            dst_ref=arrived.at[here_dp],
            send_sem=hist_sem.at[0],
            recv_sem=hist_sem.at[1],
            device_id=dp_at(d) + (im,),
            device_id_type=MESH,
        ).start()
        return carry

    lax.fori_loop(1, n_dp, send_history, 0)
    arrived[here_dp] = hist_out[here_dp]

    loads[1].wait()
    to_smem.wait()
    finish(asked, ids_sem, 1, n - 1)
    to_smem = pltpu.make_async_copy(asked, asked_s, small_sem.at[1])
    to_smem.start()
    to_smem.wait()

    def fill(out, at, d, table, idx):
        for r in range(CAP):
            out[at, r] = table[jnp.maximum(idx[d, 0, r], 0)]

    def serve(out, into, table, idx, sems, first=1, last=n):
        d0 = lax.rem(me + first, n)
        fill(out, d0, d0, table, idx)

        def one(k, carry):
            d = lax.rem(me + k, n)
            fill(out, d, d, table, idx)
            push(out, into, sems, lax.rem(me + k - 1, n))
            return carry

        lax.fori_loop(first + 1, last, one, 0)
        push(out, into, sems, lax.rem(me + last - 1, n))

    serve(fetch_out, fetch_in, tiles, asked_s, fetch_sem)
    fill(fetch_in, me, me, tiles, asked_s)

    peers = [lax.rem(im + k, nm) for k in range(1, nm)]
    finish(arrived, hist_sem, 1, n_dp - 1)
    for s in range(anchors.shape[0]):
        part[s * STEPS : (s + 1) * STEPS, :] = arrived[anchors[s]]
    rows_all, cols_here = part.shape
    width = flat.shape[1]
    quarter = rows_all // nm
    mine = pl.ds(pl.multiple_of(im * cols_here, cols_here), cols_here)
    gathers = [
        pltpu.make_async_remote_copy(
            src_ref=part,
            dst_ref=flat.at[:, mine],
            send_sem=gat_sem.at[0, i],
            recv_sem=gat_sem.at[1, i],
            device_id=(ix, iz, ic, p),
            device_id_type=MESH,
        )
        for i, p in enumerate(peers)
    ]
    for copy in gathers:
        copy.start()
    flat[:, mine] = part[...]
    for copy in gathers:
        copy.wait()

    loads[2].wait()
    loads[3].wait()
    for b in range(nm):
        rows = slice(b * quarter, (b + 1) * quarter)
        scaled, _ = center(flat[rows, :].astype(F32))
        normed[rows, :] = scaled.astype(BF16)
    heads = cols_here // DH
    for c in range(4):
        z = jnp.dot(normed[...], w_in[c], preferred_element_type=F32)
        preact[c] = z
        proj[c] = (z * sigmoid(z)).astype(BF16)

    def forward(rows, cols):
        count = count_ref[rows, :]
        scores, mask = attention_weights(proj[2, rows, cols], proj[3, rows, cols], count)
        weights = jnp.where(mask, scores * sigmoid(scores) / count, 0.0).astype(BF16)
        mixed = jnp.dot(weights, proj[1, rows, cols], preferred_element_type=F32)
        scaled, inv = center(mixed)
        return scores, mask, weights, scaled, inv

    for b in range(nm):
        for h in range(heads):
            rows = slice(b * quarter, (b + 1) * quarter)
            cols = slice(h * DH, (h + 1) * DH)
            scaled = forward(rows, cols)[3]
            gated[rows, cols] = (scaled * proj[0, rows, cols].astype(F32)).astype(BF16)

    def block(m):
        rows = pl.ds(pl.multiple_of(m * quarter, quarter), quarter)
        return jnp.dot(gated[rows, :], w_out[...], preferred_element_type=F32)

    for i, p in enumerate(peers):
        staged[i] = block(p).astype(BF16)
    copies = [
        pltpu.make_async_remote_copy(
            src_ref=staged.at[i],
            dst_ref=landed.at[i],
            send_sem=sca_sem.at[0, i],
            recv_sem=sca_sem.at[1, i],
            device_id=(ix, iz, ic, p),
            device_id_type=MESH,
        )
        for i, p in enumerate(peers)
    ]
    for copy in copies:
        copy.start()
    own = pl.ds(pl.multiple_of(im * quarter, quarter), quarter)
    total = block(im) + flat[own, :].astype(F32)
    for i, copy in enumerate(copies):
        copy.wait()
        total = total + landed[i].astype(F32)
    out_rows[...] = total
    inv_out = 1.0 / jnp.sqrt(jnp.sum(total * total, axis=-1, keepdims=True) + epsilon_unit)
    unit = total * inv_out
    unit_b = unit.astype(BF16)

    chunks, lanes = width // 128, 128
    for c in range(chunks):
        tall[pl.ds(c, quarter, stride=chunks), :] = unit[:, c * lanes : (c + 1) * lanes]
    unit_tiles = tiles.at[pl.ds(0, quarter)]
    unit_tiles[...] = tall[0 : quarter * chunks, :].reshape(quarter, chunks, lanes).astype(BF16)
    serve(unit_out, unit_in, unit_tiles, chosen_s, unit_sem)
    fill(unit_in, me, me, unit_tiles, chosen_s)

    finish(fetch_in, fetch_sem, 1, n - 1)

    def spread(ref, r):
        tall[...] = ref[:, r].astype(F32).reshape(n * chunks, lanes)

    ranks = rank[...]
    sums = jnp.zeros((1, quarter), F32)
    inverse = []
    for r in range(CAP):
        spread(fetch_in, r)
        squares = jnp.zeros((n, lanes), F32)
        for c in range(chunks):
            chunk = tall[pl.ds(c, n, stride=chunks), :]
            squares = squares + chunk * chunk
            mat[r * n : (r + 1) * n, c * lanes : (c + 1) * lanes] = chunk.astype(BF16)
        inv = 1.0 / jnp.sqrt(jnp.sum(squares, axis=-1, keepdims=True) + epsilon_unit)
        inverse.append(inv)
        dots = lax.dot_general(
            mat[r * n : (r + 1) * n, :], unit_b, OVER_COLS, preferred_element_type=F32
        )
        cos = dots * inv
        ex = jnp.where(ranks == r, jnp.exp(cos / cosine_divisor), 0.0)
        cosine[r] = cos
        expo[r] = ex
        sums = sums + jnp.sum(ex, axis=0, keepdims=True)
    valid = valid_ref[0:1, :]
    scale = valid / sums
    first = (col[...] == 0).astype(F32) * valid
    lane = lax.broadcasted_iota(jnp.int32, (n, lanes), 1)
    coef = jnp.zeros((n, lanes), F32)
    slope = jnp.zeros((quarter, width), F32)
    for r in range(CAP):
        share = expo[r] * scale - jnp.where(ranks == r, first, 0.0)
        weight = share * (inverse[r] / cosine_divisor)
        slope = slope + lax.dot_general(
            weight.astype(BF16), mat[r * n : (r + 1) * n, :], OVER_ROWS, preferred_element_type=F32
        )
        a = jnp.sum(weight, axis=-1, keepdims=True)
        b = jnp.sum(weight * cosine[r], axis=-1, keepdims=True) * inverse[r]
        coef = jnp.where(lane == r, a, coef)
        coef = jnp.where(lane == r + 8, b, coef)
    along = jnp.sum(unit * slope, axis=-1, keepdims=True)
    grad[...] = ((slope - unit * along) * inv_out).astype(BF16)
    coef_out[...] = coef.reshape(coef_out.shape)
    copies = [
        pltpu.make_async_remote_copy(
            src_ref=grad,
            dst_ref=cot.at[own, :],
            send_sem=cot_sem.at[0, i],
            recv_sem=cot_sem.at[1, i],
            device_id=(ix, iz, ic, p),
            device_id_type=MESH,
        )
        for i, p in enumerate(peers)
    ]
    for copy in copies:
        copy.start()
    send_all(coef_out, coef_in, coef_sem)
    coef_in[me] = coef_out[me]
    cot[own, :] = grad[...]
    for copy in copies:
        copy.wait()

    gated_cot[...] = lax.dot_general(
        cot[...], w_out[...], OVER_COLS, preferred_element_type=F32
    ).astype(BF16)
    for b in range(nm):
        for h in range(heads):
            rows = slice(b * quarter, (b + 1) * quarter)
            cols = slice(h * DH, (h + 1) * DH)
            count = count_ref[rows, :]
            scores, mask, weights, scaled, inv = forward(rows, cols)
            gc = gated_cot[rows, cols].astype(F32)
            d_gating = gc * scaled
            d_scaled = gc * proj[0, rows, cols].astype(F32)
            d_mixed = inv * (
                d_scaled
                - jnp.mean(d_scaled, axis=-1, keepdims=True)
                - scaled * jnp.mean(d_scaled * scaled, axis=-1, keepdims=True)
            )
            d_mixed = d_mixed.astype(BF16)
            d_weights = lax.dot_general(
                d_mixed, proj[1, rows, cols], OVER_COLS, preferred_element_type=F32
            )
            d_weights = d_weights.astype(BF16).astype(F32)
            d_values = lax.dot_general(weights, d_mixed, OVER_ROWS, preferred_element_type=F32)
            d_scores = jnp.where(
                mask, d_weights * silu_slope(scores) * (DH**-0.5) / count, 0.0
            ).astype(BF16)
            d_queries = jnp.dot(d_scores, proj[3, rows, cols], preferred_element_type=F32)
            d_keys = lax.dot_general(
                d_scores, proj[2, rows, cols], OVER_ROWS, preferred_element_type=F32
            )
            for c, d in enumerate((d_gating, d_values, d_queries, d_keys)):
                at = slice(c * cols_here + h * DH, c * cols_here + (h + 1) * DH)
                pre_cot[rows, at] = (
                    d.astype(BF16).astype(F32) * silu_slope(preact[c, rows, cols])
                ).astype(BF16)

    block_rows = width // nx
    groups = parts.shape[0]
    peer_c = (ix, iz, 1 - ic, im)
    swaps = []
    order = [lax.rem(ix + k, nx) for k in list(range(1, nx)) + [0]]
    for i, p in enumerate(order):
        at = pl.ds(pl.multiple_of(p * block_rows, block_rows), block_rows)
        res = lax.dot_general(normed[:, at], pre_cot[...], OVER_ROWS, preferred_element_type=F32)
        for c in range(4):
            parts[c, p] = (
                res[:, c * cols_here : (c + 1) * cols_here].astype(BF16).reshape(parts.shape[2:])
            )
        res = lax.dot_general(cot[:, at], gated[...], OVER_ROWS, preferred_element_type=F32)
        parts[4, p] = res.astype(BF16).reshape(parts.shape[2:])
        swaps.append(
            pltpu.make_async_remote_copy(
                src_ref=parts.at[:, p, :, 1 - ic],
                dst_ref=land_c.at[:, p],
                send_sem=c_sem.at[0, i],
                recv_sem=c_sem.at[1, i],
                device_id=peer_c,
                device_id_type=MESH,
            )
        )
        swaps[-1].start()
    copies = []
    for i in range(nx - 1):
        p = order[i]
        swaps[i].wait()
        stage_x[i] = (parts[:, p, :, ic].astype(F32) + land_c[:, p].astype(F32)).astype(BF16)
        copies.append(
            pltpu.make_async_remote_copy(
                src_ref=stage_x.at[i],
                dst_ref=land_x.at[i],
                send_sem=x_sem.at[0, i],
                recv_sem=x_sem.at[1, i],
                device_id=(p, iz, ic, im),
                device_id_type=MESH,
            )
        )
        copies[-1].start()
    swaps[nx - 1].wait()
    held = parts[:, ix, :, ic].astype(F32) + land_c[:, ix].astype(F32)
    for i, copy in enumerate(copies):
        copy.wait()
        held = held + land_x[i].astype(F32)
    stage_z[...] = held.astype(BF16)
    copies = []
    for i in range(nz - 1):
        p = lax.rem(iz + 1 + i, nz)
        copies.append(
            pltpu.make_async_remote_copy(
                src_ref=stage_z.at[:, p],
                dst_ref=land_z.at[i],
                send_sem=z_sem.at[0, i],
                recv_sem=z_sem.at[1, i],
                device_id=(ix, p, ic, im),
                device_id_type=MESH,
            )
        )
        copies[-1].start()
    held = stage_z[:, iz].astype(F32)
    for i, copy in enumerate(copies):
        copy.wait()
        held = held + land_z[i].astype(F32)
    sums_ref[...] = held

    loads[4].wait()
    finish(coef_in, coef_sem, 1, n - 1)
    finish(unit_in, unit_sem, 1, n - 1)
    wanted = asked[...].reshape(n, lanes)
    coef = coef_in[...].reshape(n, lanes)
    rows_cat = cat.shape[0]
    row = lax.broadcasted_iota(jnp.int32, (n, rows_cat), 1)
    for r in range(CAP):
        spread(unit_in, r)
        a = coef[:, r : r + 1]
        b = coef[:, r + 8 : r + 9]
        high = b.astype(BF16).astype(F32)
        span = slice(r * n, (r + 1) * n)
        for c in range(chunks):
            chunk = tall[pl.ds(c, n, stride=chunks), :]
            mat[span, c * lanes : (c + 1) * lanes] = (chunk * a).astype(BF16)
        side[span, :] = jnp.where(
            lane == 0, high, jnp.where(lane == 1, b - high, 0.0)
        ).astype(BF16)
        hot[span, :] = (wanted[:, r : r + 1] == row).astype(F32).astype(BF16)
    both = lax.dot_general(hot[...], side[...], OVER_ROWS, preferred_element_type=F32)
    b_row = both[:, 0:1] + both[:, 1:2]
    for c in range(0, width, 256):
        res = lax.dot_general(hot[...], mat[:, c : c + 256], OVER_ROWS, preferred_element_type=F32)
        cat_grad_ref[:, c : c + 256] = res - b_row * cat[:, c : c + 256].astype(F32)

    finish(want_out, ids_sem, 0, n - 1)
    finish(hist_out, hist_sem, 0, n_dp - 1)
    finish(fetch_out, fetch_sem, 0, n - 1)
    finish(unit_out, unit_sem, 0, n - 1)
    finish(coef_out, coef_sem, 0, n - 1)


ALL = ("x", "z", "c", "mp")
DP = ("x", "z", "c")
NX, NZ, NC, NM = 4, 8, 2, 4


def step(seq_for, anchors, owners_t, rows_t, counts, valid, history, tiles, catalogue, w_in, w_out):
    n_dp = NX * NZ * NC
    n = n_dp * NM
    seqs, steps, cols = history.shape
    rows_all = seqs * steps
    rows_cat, width = catalogue.shape
    quarter = rows_all // NM
    chunks = width // 128
    rows_out = width // n_dp
    dma = pltpu.SemaphoreType.DMA
    V = pltpu.VMEM
    I32 = jnp.int32
    anyw = pl.BlockSpec(memory_space=pl.ANY)
    message = (n, CAP, chunks, 128)
    scratch = [
        V(history.shape, BF16), V((n_dp, steps, cols), BF16), V((n_dp, steps, cols), BF16),
        V(tiles.shape, BF16), V(catalogue.shape, BF16), V(w_in.shape, BF16), V(w_out.shape, BF16), dma((5,)),
        V((n, 128), I32), V((n, 128), I32), V((n, quarter), I32), V((n, quarter), I32),
        V((n, 1, 128), I32), V((n, 1, 128), I32), V((n, 1, 128), I32),
        pltpu.SMEM((n, 1, 128), I32), pltpu.SMEM((n, 1, 128), I32), dma((2,)),
        V(message, BF16), V(message, BF16), V(message, BF16), V(message, BF16),
        V((n, 1, 128), F32), V((n, 1, 128), F32),
        V((rows_all, cols), BF16), V((rows_all, width), BF16), V((rows_all, width), BF16),
        V((4, rows_all, cols), F32), V((4, rows_all, cols), BF16), V((rows_all, cols), BF16),
        V((NM - 1, quarter, width), BF16), V((NM - 1, quarter, width), BF16),
        V((quarter, width), F32), V((n * chunks, 128), F32), V((CAP * n, width), BF16),
        V((CAP, n, quarter), F32), V((CAP, n, quarter), F32), V((quarter, width), BF16),
        V((rows_all, width), BF16), V((rows_all, cols), BF16), V((rows_all, 4 * cols), BF16),
        V((5, NX, NZ, NC, rows_out, cols), BF16), V((5, NX, NZ, rows_out, cols), BF16),
        V((NX - 1, 5, NZ, rows_out, cols), BF16), V((NX - 1, 5, NZ, rows_out, cols), BF16),
        V((5, NZ, rows_out, cols), BF16), V((NZ - 1, 5, rows_out, cols), BF16),
        V((CAP * n, rows_cat), BF16), V((CAP * n, 128), BF16),
        dma((2,)), dma((2,)), dma((2,)), dma((2,)), dma((2,)),
        dma((2, NM - 1)), dma((2, NM - 1)), dma((2, NM - 1)),
        dma((2, NX)), dma((2, NX - 1)), dma((2, NZ - 1)),
    ]
    return pl.pallas_call(
        step_kernel,
        out_shape=(sds((rows_cat, width), F32), sds((5, rows_out, cols), F32)),
        in_specs=[SM, SM, VM, VM, VM, VM] + [anyw] * 5,
        out_specs=(VM, VM),
        scratch_shapes=scratch,
        compiler_params=params(collective_id=0, has_side_effects=True),
        name="step",
    )(seq_for, anchors, owners_t, rows_t, counts, valid, history, tiles, catalogue, w_in, w_out)


def per_device(history, lengths, source, owners, item_rows, catalogue, w_in, w_out):
    n_dp = NX * NZ * NC
    here_dp = (lax.axis_index("x") * NZ + lax.axis_index("z")) * NC + lax.axis_index("c")
    here_mp = lax.axis_index("mp")
    seq_dev, steps_n, _ = history.shape
    seq_total = source.shape[0]
    rows_all = seq_dev * steps_n
    quarter = rows_all // NM

    slot_ids = jnp.arange(seq_dev, dtype=jnp.int32)
    my_seqs = here_dp * seq_dev + slot_ids
    places = jnp.arange(seq_total, dtype=jnp.int32)
    target = jnp.sum(jnp.where(source[None, :] == my_seqs[:, None], places[None, :], 0), axis=1)
    dests = jnp.arange(n_dp, dtype=jnp.int32)
    seq_for = jnp.sum(
        jnp.where((target // seq_dev)[None, :] == dests[:, None], slot_ids[None, :], 0), axis=1
    )
    taken = lax.dynamic_slice_in_dim(source, here_dp * seq_dev, seq_dev, 0)
    counts = jnp.sum(jnp.where(places[None, :] == taken[:, None], lengths[None, :], 0), axis=1)
    per_row = jnp.broadcast_to(counts[:, None], (seq_dev, steps_n)).reshape(rows_all)
    spot = jnp.arange(rows_all, dtype=jnp.int32) % steps_n
    valid = lax.dynamic_slice_in_dim((spot < per_row).astype(F32), here_mp * quarter, quarter, 0)
    tiles = catalogue.reshape(catalogue.shape[0], catalogue.shape[1] // 128, 128)
    cat_grad, sums = step(
        seq_for,
        taken // seq_dev,
        owners.T,
        item_rows.T,
        per_row.astype(F32)[:, None],
        jnp.broadcast_to(valid[None, :], (8, quarter)),
        history,
        tiles,
        catalogue,
        w_in,
        w_out,
    )
    return (sums[:4], sums[4].T, cat_grad)


def solution(mesh):
    split = Mesh(mesh.devices.reshape(NX, NZ, NC, NM), ALL)
    placed = (
        P(DP, None, "mp"),
        P(),
        P(),
        P(ALL, None),
        P(ALL, None),
        P(ALL, None),
        P(None, None, "mp"),
        P("mp", None),
    )
    return jax.shard_map(
        per_device,
        mesh=split,
        in_specs=placed,
        out_specs=(P(None, DP, "mp"), P("mp", DP), P(ALL, None)),
        check_vma=False,
    )
```

time: 695 us -> 234 us (0.34)
  waiting for transfers between devices: 419 us -> 0 us
  Pallas kernels: 0 us -> 215 us
  local copies, waits for them, and re-layouts: 123 us -> 10.3 us
  other arithmetic: 55.5 us -> 3.65 us
  starting transfers between devices: 47.7 us -> 0 us
  matrix products: 21.9 us -> 0 us
  between operations: 16 us -> 0.66 us
    pallas_call x0 -> x1, Pallas kernels: none -> 215 us  [step(): pl.pallas_call(step_kernel, out_shape=(sds((rows_cat, width), F32), sds((...]
    unnamed x6 -> x0, waiting for transfers between devices: 161 us -> none
    reduce_scatter x1 -> x0, waiting for transfers between devices: 109 us -> none  [per_device(): lax.psum_scatter(w_out_part, 'dp', scatter_dimension=1, tiled=True)]
    all_to_all x7 -> x0, waiting for transfers between devices: 69.5 us -> none  [the longest x1 30.3 us: per_device(): lax.all_to_all(looked, 'dp', split_axis=0, concat_axis=0, tiled=True)]
    all_gather x2 -> x0, waiting for transfers between devices: 53.8 us -> none  [the longest x1 28.8 us: per_device(): lax.all_gather(out_grad.astype(jnp.bfloat16), 'mp', axis=0, tiled=True)]
    all_to_all x7 -> x0, starting transfers between devices: 47 us -> none  [the longest x1 13 us: per_device(): lax.all_to_all(wanted, 'dp', split_axis=0, concat_axis=0, tiled=True)]
    gather x13 -> x0, local copies, waits for them, and re-layouts: 42.3 us -> none  [the longest x2 12.1 us: per_device(): jnp.take(catalogue, incoming_flat, axis=0)]
    psum x1 -> x0, waiting for transfers between devices: 25.9 us -> none  [per_device(): summed = lax.psum(partial_out, 'mp')]
  transfers between devices with their start and end apart: 12 -> 0, of which waited for: 11 -> 0; matrix products, arithmetic and copies ran while one was open for 20% -> 0% of each run, Pallas kernels for 0% -> 0%
where the time goes in v2:
time: 234 us; the launch traced here: 230 us
  Pallas kernels  215 us (92%)
  local copies, waits for them, and re-layouts  10.3 us (4%)
  other arithmetic  3.65 us (2%)
    pallas_call x1, Pallas kernels, step(): pl.pallas_call(step_kernel, out_shape=(sds((rows_cat, width), F32), sds((...  215 us
    unnamed x2, local copies, waits for them, and re-layouts  5.63 us

profile of v2, /device:TPU:1, one launch (start us, length us, event | category | flops | bytes accessed | tf_op | source)
XLA Modules:
  0.0 229.5 jit_solution(3395060453353030268)
XLA Ops:
  0.7 0.9 select_reduce_fusion.1
  1.5 0.6 select_reduce_fusion.2.seq_for
  2.1 1.3 and_select_fusion
  3.4 0.9 select_reduce_fusion
  4.3 0.1 broadcast_in_dim.63
  4.4 0.1 reshape.49
  4.4 0.1 dynamic_slice.7
  4.5 0.6 broadcast_in_dim.64.valid_ref
  5.1 0.1 broadcast_in_dim.62
  5.2 1.0 convert_element_type.20.count_ref
  6.2 2.5 %copy.13 = bf16[64,8,8,128]{3,2,1,0:T(8,128)(2,1)} copy(bf16[64,8,8,128]{3,1,2,0:T(8,128)(2,1)} %bitcast.8) | data formatting | bytes 2097152
  8.7 214.9 %step.1 = (f32[512,1024]{1,0:T(8,128)}, f32[5,16,256]{2,1,0:T(8,128)}) custom-call(s32[64]{0:T(128)} %select_reduce_fusion.2.seq_for, s32[16]{0:T(128)} %get-tuple-element.7.anchors, s32[8,128]{1,0:T(8,128)} %bitcast.10, s32[8,128]{1,0:T(8,128)} %bitcast.11, f32[512,1]{1,0:T(8,128)} %convert_element_type.20.count_ref, f32[8,128]{1,0:T(8,128)} %broadcast_in_dim.64.valid_ref, ...), custom_call_target="tpu_custom_call" | custom-call | tf_op jit(solution)/shard_map/step/pallas_call | solution.py:554
  223.6 1.3 slice_bitcast_fusion
  224.9 1.5 slice.6
  226.4 3.2 %copy.15 = f32[512,1024]{1,0:T(8,128)} copy(f32[512,1024]{1,0:T(8,128)} %get-tuple-element.14) | data formatting | bytes 4194304
  (4 shorter events, 0.0 us)

commit v3 on v2

--- a/solution.py
+++ b/solution.py
@@ -35,8 +35,11 @@
     named = jnp.zeros((owners_n, events), F32)
     rows = jnp.zeros((owners_n, events), jnp.int32)
     cols = jnp.zeros((owners_n, events), jnp.int32)
+    own = own_ref[...]
+    core = lax.rem(lax.div(own, NM), NC)
+    own = core * (owners_n // NC) + lax.div(own, NM * NC) * NM + lax.rem(own, NM)
     for j in range(own_ref.shape[0]):
-        mask = own_ref[j : j + 1, :] == who
+        mask = own[j : j + 1, :] == who
         named = jnp.where(mask, 1.0, named)
         rows = jnp.where(mask, row_ref[j : j + 1, :], rows)
         cols = jnp.where(mask, j, cols)
@@ -97,10 +100,10 @@
 
 
 def step_kernel(
-    seq_for, anchors, owners_ref, rows_ref, count_ref, valid_ref,
-    history_hbm, tiles_hbm, cat_hbm, w_in_hbm, w_out_hbm,
+    source_s, lengths_s, source_ref, owners_ref, rows_ref,
+    history_hbm, cat_hbm, w_in_hbm, w_out_hbm,
     cat_grad_ref, sums_ref,
-    hist, hist_out, arrived, tiles, cat, w_in, w_out, load_sem,
+    count_ref, seq_v, seq_s, hist, hist_out, arrived, tiles, cat, w_in, w_out, load_sem,
     want, event, rank, col, chosen_v, want_out, asked, asked_s, chosen_s, small_sem,
     fetch_out, fetch_in, unit_out, unit_in, coef_out, coef_in,
     part, flat, normed, preact, proj, gated, staged, landed,
@@ -113,19 +116,26 @@
     nx, nz, nc, nm = NX, NZ, NC, NM
     n = nx * nz * nc * nm
     here_dp = (ix * nz + iz) * nc + ic
-    me = here_dp * nm + im
     n_dp = nx * nz * nc
+    chips = nx * nz * nm
+    chip = (ix * nz + iz) * nm + im
+    me = ic * chips + chip
+    cores = (ic, 1 - ic)
+    bases = [pl.multiple_of(core * chips, chips) for core in cores]
 
     def dp_at(d):
         return (lax.div(d, nz * nc), lax.rem(lax.div(d, nc), nz), lax.rem(d, nc))
 
-    def device(d):
-        return dp_at(lax.div(d, nm)) + (lax.rem(d, nm),)
+    def device(core, q):
+        return (lax.div(q, nz * nm), lax.rem(lax.div(q, nm), nz), core, lax.rem(q, nm))
+
+    def chip_at(k):
+        return lax.rem(chip + k, chips)
 
     loads = [
         pltpu.make_async_copy(a, b, load_sem.at[i])
         for i, (a, b) in enumerate(
-            [(history_hbm, hist), (tiles_hbm, tiles), (w_in_hbm, w_in), (w_out_hbm, w_out), (cat_hbm, cat)]
+            [(history_hbm, hist), (cat_hbm, cat), (w_in_hbm, w_in), (w_out_hbm, w_out)]
         )
     ]
     for load in loads:
@@ -133,43 +143,63 @@
 
     barrier = pltpu.get_barrier_semaphore()
 
-    def greet(k, carry):
+    def greet(core, k):
         pl.semaphore_signal(
-            barrier, inc=1, device_id=device(lax.rem(me + k, n)), device_id_type=MESH
-        )
-        return carry
-
-    lax.fori_loop(1, n, greet, 0)
+            barrier, inc=1, device_id=device(core, chip_at(k)), device_id_type=MESH
+        )
+
+    def to_both(act):
+        act(cores[1], 0)
+        for core in cores:
+            act(core, 1)
+
+        def one(k, carry):
+            for core in cores:
+                act(core, k)
+            return carry
+
+        lax.fori_loop(2, chips, one, 0, unroll=6)
+
+    to_both(greet)
 
     slots_kernel(owners_ref, rows_ref, want, event, rank, col)
     want_out[...] = want[...].reshape(want_out.shape)
     chosen_v[...] = event[...].reshape(chosen_v.shape)
     to_smem = pltpu.make_async_copy(chosen_v, chosen_s, small_sem.at[0])
     to_smem.start()
+    from_here = lax.div(source_ref[...], SEQ_DEV) == here_dp
+    local = jnp.where(from_here, lax.rem(source_ref[...], SEQ_DEV), 0)
+    local = jnp.max(local, axis=1, keepdims=True)
+    seq_v[...] = jnp.broadcast_to(local, (n_dp, 128)).reshape(seq_v.shape)
+    seq_copy = pltpu.make_async_copy(seq_v, seq_s, small_sem.at[1])
+    seq_copy.start()
+    lengths = [lengths_s[source_s[here_dp * SEQ_DEV + i]] for i in range(SEQ_DEV)]
+    for i, length in enumerate(lengths):
+        count_ref[i * STEPS : (i + 1) * STEPS, :] = jnp.full((STEPS, 1), length).astype(F32)
     loads[0].wait()
+    seq_copy.wait()
 
     def stage(d, carry):
-        hist_out[d] = hist[seq_for[d]]
+        hist_out[d] = hist[seq_s[d, 0, 0]]
         return carry
 
     lax.fori_loop(0, n_dp, stage, 0, unroll=4)
+    loads[1].wait()
+    chunks, lanes = cat.shape[1] // 128, 128
+    for i in range(cat.shape[0] // chips):
+        rows = slice(i * chips, (i + 1) * chips)
+        for c in range(chunks):
+            tall[pl.ds(c, chips, stride=chunks), :] = cat[rows, c * lanes : (c + 1) * lanes].astype(F32)
+        tiles[rows] = tall[...].reshape(chips, chunks, lanes).astype(BF16)
     pl.semaphore_wait(barrier, n - 1)
 
-    def send_all(src, dst, sems, first=1, last=n):
-        def one(k, carry):
-            d = lax.rem(me + k, n)
-            push(src, dst, sems, d)
-            return carry
-
-        lax.fori_loop(first, last, one, 0)
-
-    def push(src, dst, sems, d):
+    def push(src, dst, sems, core, q):
         pltpu.make_async_remote_copy(
-            src_ref=src.at[d],
+            src_ref=src.at[core * chips + q],
             dst_ref=dst.at[me],
             send_sem=sems.at[0],
             recv_sem=sems.at[1],
-            device_id=device(d),
+            device_id=device(core, q),
             device_id_type=MESH,
         ).start()
 
@@ -177,7 +207,7 @@
         block = ref.at[pl.ds(0, count)]
         pltpu.make_async_copy(block, block, sems.at[which]).wait()
 
-    send_all(want_out, asked, ids_sem)
+    to_both(lambda core, k: push(want_out, asked, ids_sem, core, chip_at(k)))
     asked[me] = want_out[me]
 
     def send_history(k, carry):
@@ -195,37 +225,38 @@
     lax.fori_loop(1, n_dp, send_history, 0)
     arrived[here_dp] = hist_out[here_dp]
 
-    loads[1].wait()
     to_smem.wait()
     finish(asked, ids_sem, 1, n - 1)
     to_smem = pltpu.make_async_copy(asked, asked_s, small_sem.at[1])
     to_smem.start()
     to_smem.wait()
 
-    def fill(out, at, d, table, idx):
+    def fill(out, d, table, idx):
         for r in range(CAP):
-            out[at, r] = table[jnp.maximum(idx[d, 0, r], 0)]
-
-    def serve(out, into, table, idx, sems, first=1, last=n):
-        d0 = lax.rem(me + first, n)
-        fill(out, d0, d0, table, idx)
+            out[d, r] = table[jnp.maximum(idx[d, 0, r], 0)]
+
+    def serve(out, into, table, idx, sems, core, first, last, unroll):
+        fill(out, core * chips + chip_at(first), table, idx)
 
         def one(k, carry):
-            d = lax.rem(me + k, n)
-            fill(out, d, d, table, idx)
-            push(out, into, sems, lax.rem(me + k - 1, n))
+            fill(out, core * chips + chip_at(k), table, idx)
+            push(out, into, sems, core, chip_at(k - 1))
             return carry
 
-        lax.fori_loop(first + 1, last, one, 0)
-        push(out, into, sems, lax.rem(me + last - 1, n))
-
-    serve(fetch_out, fetch_in, tiles, asked_s, fetch_sem)
-    fill(fetch_in, me, me, tiles, asked_s)
+        lax.fori_loop(first + 1, last, one, 0, unroll=unroll)
+        push(out, into, sems, core, chip_at(last - 1))
+
+    def serve_rows(part, first, last, unroll):
+        serve(fetch_out, fetch_in, tiles, asked_s, fetch_sem.at[part], cores[part], first, last, unroll)
+
+    serve_rows(0, 1, chips, 6)
+    fill(fetch_out, me, tiles, asked_s)
+    fetch_in[me] = fetch_out[me]
 
     peers = [lax.rem(im + k, nm) for k in range(1, nm)]
     finish(arrived, hist_sem, 1, n_dp - 1)
-    for s in range(anchors.shape[0]):
-        part[s * STEPS : (s + 1) * STEPS, :] = arrived[anchors[s]]
+    for s in range(SEQ_DEV):
+        part[s * STEPS : (s + 1) * STEPS, :] = arrived[lax.div(source_s[here_dp * SEQ_DEV + s], SEQ_DEV)]
     rows_all, cols_here = part.shape
     width = flat.shape[1]
     quarter = rows_all // nm
@@ -243,6 +274,7 @@
     ]
     for copy in gathers:
         copy.start()
+    serve_rows(1, 0, chips // 2, 7)
     flat[:, mine] = part[...]
     for copy in gathers:
         copy.wait()
@@ -293,6 +325,7 @@
     ]
     for copy in copies:
         copy.start()
+    serve_rows(1, chips // 2, chips, 7)
     own = pl.ds(pl.multiple_of(im * quarter, quarter), quarter)
     total = block(im) + flat[own, :].astype(F32)
     for i, copy in enumerate(copies):
@@ -303,58 +336,72 @@
     unit = total * inv_out
     unit_b = unit.astype(BF16)
 
-    chunks, lanes = width // 128, 128
     for c in range(chunks):
         tall[pl.ds(c, quarter, stride=chunks), :] = unit[:, c * lanes : (c + 1) * lanes]
     unit_tiles = tiles.at[pl.ds(0, quarter)]
-    unit_tiles[...] = tall[0 : quarter * chunks, :].reshape(quarter, chunks, lanes).astype(BF16)
-    serve(unit_out, unit_in, unit_tiles, chosen_s, unit_sem)
-    fill(unit_in, me, me, unit_tiles, chosen_s)
-
-    finish(fetch_in, fetch_sem, 1, n - 1)
-
-    def spread(ref, r):
-        tall[...] = ref[:, r].astype(F32).reshape(n * chunks, lanes)
-
-    ranks = rank[...]
+    unit_tiles[...] = tall[...].reshape(quarter, chunks, lanes).astype(BF16)
+
+    def serve_units(part, first, last, unroll):
+        serve(unit_out, unit_in, unit_tiles, chosen_s, unit_sem.at[part], cores[part], first, last, unroll)
+
+    serve_units(0, 1, chips, 6)
+    fill(unit_out, me, unit_tiles, chosen_s)
+    unit_in[me] = unit_out[me]
+
+    def spread(ref, base, r):
+        tall[...] = ref[pl.ds(base, chips), r].astype(F32).reshape(chips * chunks, lanes)
+
     sums = jnp.zeros((1, quarter), F32)
-    inverse = []
-    for r in range(CAP):
-        spread(fetch_in, r)
-        squares = jnp.zeros((n, lanes), F32)
-        for c in range(chunks):
-            chunk = tall[pl.ds(c, n, stride=chunks), :]
-            squares = squares + chunk * chunk
-            mat[r * n : (r + 1) * n, c * lanes : (c + 1) * lanes] = chunk.astype(BF16)
-        inv = 1.0 / jnp.sqrt(jnp.sum(squares, axis=-1, keepdims=True) + epsilon_unit)
-        inverse.append(inv)
-        dots = lax.dot_general(
-            mat[r * n : (r + 1) * n, :], unit_b, OVER_COLS, preferred_element_type=F32
-        )
-        cos = dots * inv
-        ex = jnp.where(ranks == r, jnp.exp(cos / cosine_divisor), 0.0)
-        cosine[r] = cos
-        expo[r] = ex
-        sums = sums + jnp.sum(ex, axis=0, keepdims=True)
-    valid = valid_ref[0:1, :]
+    inverse = {}
+    for p, base in enumerate(bases):
+        finish(fetch_in, fetch_sem.at[p], 1, chips - 1 + p)
+        ranks = rank[pl.ds(base, chips), :]
+        for r in range(CAP):
+            i = p * CAP + r
+            spread(fetch_in, base, r)
+            squares = jnp.zeros((chips, lanes), F32)
+            for c in range(chunks):
+                chunk = tall[pl.ds(c, chips, stride=chunks), :]
+                squares = squares + chunk * chunk
+                mat[i * chips : (i + 1) * chips, c * lanes : (c + 1) * lanes] = chunk.astype(BF16)
+            inv = 1.0 / jnp.sqrt(jnp.sum(squares, axis=-1, keepdims=True) + epsilon_unit)
+            inverse[i] = inv
+            dots = lax.dot_general(
+                mat[i * chips : (i + 1) * chips, :], unit_b, OVER_COLS, preferred_element_type=F32
+            )
+            cos = dots * inv
+            ex = jnp.where(ranks == r, jnp.exp(cos / cosine_divisor), 0.0)
+            cosine[i] = cos
+            expo[i] = ex
+            sums = sums + jnp.sum(ex, axis=0, keepdims=True)
+    lane_q = lax.broadcasted_iota(jnp.int32, (1, quarter), 1)
+    valid = jnp.zeros((1, quarter), F32)
+    for i in range(quarter // STEPS):
+        length = lengths_s[source_s[here_dp * SEQ_DEV + im * (quarter // STEPS) + i]]
+        inside = (lane_q >= i * STEPS) & (lane_q < (i + 1) * STEPS) & (lane_q - i * STEPS < length)
+        valid = jnp.where(inside, 1.0, valid)
     scale = valid / sums
-    first = (col[...] == 0).astype(F32) * valid
-    lane = lax.broadcasted_iota(jnp.int32, (n, lanes), 1)
-    coef = jnp.zeros((n, lanes), F32)
+    lane = lax.broadcasted_iota(jnp.int32, (chips, lanes), 1)
     slope = jnp.zeros((quarter, width), F32)
-    for r in range(CAP):
-        share = expo[r] * scale - jnp.where(ranks == r, first, 0.0)
-        weight = share * (inverse[r] / cosine_divisor)
-        slope = slope + lax.dot_general(
-            weight.astype(BF16), mat[r * n : (r + 1) * n, :], OVER_ROWS, preferred_element_type=F32
-        )
-        a = jnp.sum(weight, axis=-1, keepdims=True)
-        b = jnp.sum(weight * cosine[r], axis=-1, keepdims=True) * inverse[r]
-        coef = jnp.where(lane == r, a, coef)
-        coef = jnp.where(lane == r + 8, b, coef)
+    for p, base in enumerate(bases):
+        ranks = rank[pl.ds(base, chips), :]
+        first = (col[pl.ds(base, chips), :] == 0).astype(F32) * valid
+        coef = jnp.zeros((chips, lanes), F32)
+        for r in range(CAP):
+            i = p * CAP + r
+            share = expo[i] * scale - jnp.where(ranks == r, first, 0.0)
+            weight = share * (inverse[i] / cosine_divisor)
+            slope = slope + lax.dot_general(
+                weight.astype(BF16), mat[i * chips : (i + 1) * chips, :], OVER_ROWS,
+                preferred_element_type=F32,
+            )
+            a = jnp.sum(weight, axis=-1, keepdims=True)
+            b = jnp.sum(weight * cosine[i], axis=-1, keepdims=True) * inverse[i]
+            coef = jnp.where(lane == r, a, coef)
+            coef = jnp.where(lane == r + 8, b, coef)
+        coef_out[pl.ds(base, chips)] = coef.reshape(chips, 1, lanes)
     along = jnp.sum(unit * slope, axis=-1, keepdims=True)
     grad[...] = ((slope - unit * along) * inv_out).astype(BF16)
-    coef_out[...] = coef.reshape(coef_out.shape)
     copies = [
         pltpu.make_async_remote_copy(
             src_ref=grad,
@@ -368,7 +415,8 @@
     ]
     for copy in copies:
         copy.start()
-    send_all(coef_out, coef_in, coef_sem)
+    to_both(lambda core, k: push(coef_out, coef_in, coef_sem, core, chip_at(k)))
+    serve_units(1, 0, chips, 1)
     coef_in[me] = coef_out[me]
     cot[own, :] = grad[...]
     for copy in copies:
@@ -471,51 +519,61 @@
             )
         )
         copies[-1].start()
+
+    finish(coef_in, coef_sem, 1, n - 1)
+    rows_cat = cat.shape[0]
+    row = lax.broadcasted_iota(jnp.int32, (chips, rows_cat), 1)
+
+    def catalogue_half(p):
+        base = bases[p]
+        finish(unit_in, unit_sem.at[p], 1, chips - 1 + p)
+        wanted = asked[pl.ds(base, chips)].reshape(chips, lanes)
+        coef = coef_in[pl.ds(base, chips)].reshape(chips, lanes)
+        half = slice(p * CAP * chips, (p + 1) * CAP * chips)
+        for r in range(CAP):
+            spread(unit_in, base, r)
+            a = coef[:, r : r + 1]
+            b = coef[:, r + 8 : r + 9]
+            high = b.astype(BF16).astype(F32)
+            span = slice((p * CAP + r) * chips, (p * CAP + r + 1) * chips)
+            for c in range(chunks):
+                chunk = tall[pl.ds(c, chips, stride=chunks), :]
+                mat[span, c * lanes : (c + 1) * lanes] = (chunk * a).astype(BF16)
+            side[span, :] = jnp.where(
+                lane == 0, high, jnp.where(lane == 1, b - high, 0.0)
+            ).astype(BF16)
+            hot[span, :] = (wanted[:, r : r + 1] == row).astype(F32).astype(BF16)
+        both = lax.dot_general(hot[half, :], side[half, :], OVER_ROWS, preferred_element_type=F32)
+        b_row = both[:, 0:1] + both[:, 1:2]
+        for c in range(0, width, 256):
+            at = slice(c, c + 256)
+            res = lax.dot_general(hot[half, :], mat[half, at], OVER_ROWS, preferred_element_type=F32)
+            res = res - b_row * cat[:, at].astype(F32)
+            cat_grad_ref[:, at] = res if p == 0 else cat_grad_ref[:, at] + res
+
+    catalogue_half(0)
     held = stage_z[:, iz].astype(F32)
     for i, copy in enumerate(copies):
         copy.wait()
         held = held + land_z[i].astype(F32)
     sums_ref[...] = held
-
-    loads[4].wait()
-    finish(coef_in, coef_sem, 1, n - 1)
-    finish(unit_in, unit_sem, 1, n - 1)
-    wanted = asked[...].reshape(n, lanes)
-    coef = coef_in[...].reshape(n, lanes)
-    rows_cat = cat.shape[0]
-    row = lax.broadcasted_iota(jnp.int32, (n, rows_cat), 1)
-    for r in range(CAP):
-        spread(unit_in, r)
-        a = coef[:, r : r + 1]
-        b = coef[:, r + 8 : r + 9]
-        high = b.astype(BF16).astype(F32)
-        span = slice(r * n, (r + 1) * n)
-        for c in range(chunks):
-            chunk = tall[pl.ds(c, n, stride=chunks), :]
-            mat[span, c * lanes : (c + 1) * lanes] = (chunk * a).astype(BF16)
-        side[span, :] = jnp.where(
-            lane == 0, high, jnp.where(lane == 1, b - high, 0.0)
-        ).astype(BF16)
-        hot[span, :] = (wanted[:, r : r + 1] == row).astype(F32).astype(BF16)
-    both = lax.dot_general(hot[...], side[...], OVER_ROWS, preferred_element_type=F32)
-    b_row = both[:, 0:1] + both[:, 1:2]
-    for c in range(0, width, 256):
-        res = lax.dot_general(hot[...], mat[:, c : c + 256], OVER_ROWS, preferred_element_type=F32)
-        cat_grad_ref[:, c : c + 256] = res - b_row * cat[:, c : c + 256].astype(F32)
+    catalogue_half(1)
 
     finish(want_out, ids_sem, 0, n - 1)
     finish(hist_out, hist_sem, 0, n_dp - 1)
-    finish(fetch_out, fetch_sem, 0, n - 1)
-    finish(unit_out, unit_sem, 0, n - 1)
+    for p in range(nc):
+        finish(fetch_out, fetch_sem.at[p], 0, chips - 1 + p)
+        finish(unit_out, unit_sem.at[p], 0, chips - 1 + p)
     finish(coef_out, coef_sem, 0, n - 1)
 
 
 ALL = ("x", "z", "c", "mp")
 DP = ("x", "z", "c")
 NX, NZ, NC, NM = 4, 8, 2, 4
-
-
-def step(seq_for, anchors, owners_t, rows_t, counts, valid, history, tiles, catalogue, w_in, w_out):
+SEQ_DEV = 16
+
+
+def step(source, lengths, source_2d, owners_t, rows_t, history, catalogue, w_in, w_out):
     n_dp = NX * NZ * NC
     n = n_dp * NM
     seqs, steps, cols = history.shape
@@ -530,8 +588,9 @@
     anyw = pl.BlockSpec(memory_space=pl.ANY)
     message = (n, CAP, chunks, 128)
     scratch = [
+        V((rows_all, 1), F32), V((n_dp, 1, 128), I32), pltpu.SMEM((n_dp, 1, 128), I32),
         V(history.shape, BF16), V((n_dp, steps, cols), BF16), V((n_dp, steps, cols), BF16),
-        V(tiles.shape, BF16), V(catalogue.shape, BF16), V(w_in.shape, BF16), V(w_out.shape, BF16), dma((5,)),
+        V((rows_cat, chunks, 128), BF16), V(catalogue.shape, BF16), V(w_in.shape, BF16), V(w_out.shape, BF16), dma((4,)),
         V((n, 128), I32), V((n, 128), I32), V((n, quarter), I32), V((n, quarter), I32),
         V((n, 1, 128), I32), V((n, 1, 128), I32), V((n, 1, 128), I32),
         pltpu.SMEM((n, 1, 128), I32), pltpu.SMEM((n, 1, 128), I32), dma((2,)),
@@ -540,60 +599,36 @@
         V((rows_all, cols), BF16), V((rows_all, width), BF16), V((rows_all, width), BF16),
         V((4, rows_all, cols), F32), V((4, rows_all, cols), BF16), V((rows_all, cols), BF16),
         V((NM - 1, quarter, width), BF16), V((NM - 1, quarter, width), BF16),
-        V((quarter, width), F32), V((n * chunks, 128), F32), V((CAP * n, width), BF16),
-        V((CAP, n, quarter), F32), V((CAP, n, quarter), F32), V((quarter, width), BF16),
+        V((quarter, width), F32), V((n // NC * chunks, 128), F32), V((CAP * n, width), BF16),
+        V((NC * CAP, n // NC, quarter), F32), V((NC * CAP, n // NC, quarter), F32), V((quarter, width), BF16),
         V((rows_all, width), BF16), V((rows_all, cols), BF16), V((rows_all, 4 * cols), BF16),
         V((5, NX, NZ, NC, rows_out, cols), BF16), V((5, NX, NZ, rows_out, cols), BF16),
         V((NX - 1, 5, NZ, rows_out, cols), BF16), V((NX - 1, 5, NZ, rows_out, cols), BF16),
         V((5, NZ, rows_out, cols), BF16), V((NZ - 1, 5, rows_out, cols), BF16),
         V((CAP * n, rows_cat), BF16), V((CAP * n, 128), BF16),
-        dma((2,)), dma((2,)), dma((2,)), dma((2,)), dma((2,)),
+        dma((2,)), dma((2,)), dma((NC, 2)), dma((NC, 2)), dma((2,)),
         dma((2, NM - 1)), dma((2, NM - 1)), dma((2, NM - 1)),
         dma((2, NX)), dma((2, NX - 1)), dma((2, NZ - 1)),
     ]
     return pl.pallas_call(
         step_kernel,
         out_shape=(sds((rows_cat, width), F32), sds((5, rows_out, cols), F32)),
-        in_specs=[SM, SM, VM, VM, VM, VM] + [anyw] * 5,
+        in_specs=[SM, SM, VM, VM, VM] + [anyw] * 4,
         out_specs=(VM, VM),
         scratch_shapes=scratch,
         compiler_params=params(collective_id=0, has_side_effects=True),
         name="step",
-    )(seq_for, anchors, owners_t, rows_t, counts, valid, history, tiles, catalogue, w_in, w_out)
+    )(source, lengths, source_2d, owners_t, rows_t, history, catalogue, w_in, w_out)
 
 
 def per_device(history, lengths, source, owners, item_rows, catalogue, w_in, w_out):
-    n_dp = NX * NZ * NC
-    here_dp = (lax.axis_index("x") * NZ + lax.axis_index("z")) * NC + lax.axis_index("c")
-    here_mp = lax.axis_index("mp")
-    seq_dev, steps_n, _ = history.shape
-    seq_total = source.shape[0]
-    rows_all = seq_dev * steps_n
-    quarter = rows_all // NM
-
-    slot_ids = jnp.arange(seq_dev, dtype=jnp.int32)
-    my_seqs = here_dp * seq_dev + slot_ids
-    places = jnp.arange(seq_total, dtype=jnp.int32)
-    target = jnp.sum(jnp.where(source[None, :] == my_seqs[:, None], places[None, :], 0), axis=1)
-    dests = jnp.arange(n_dp, dtype=jnp.int32)
-    seq_for = jnp.sum(
-        jnp.where((target // seq_dev)[None, :] == dests[:, None], slot_ids[None, :], 0), axis=1
-    )
-    taken = lax.dynamic_slice_in_dim(source, here_dp * seq_dev, seq_dev, 0)
-    counts = jnp.sum(jnp.where(places[None, :] == taken[:, None], lengths[None, :], 0), axis=1)
-    per_row = jnp.broadcast_to(counts[:, None], (seq_dev, steps_n)).reshape(rows_all)
-    spot = jnp.arange(rows_all, dtype=jnp.int32) % steps_n
-    valid = lax.dynamic_slice_in_dim((spot < per_row).astype(F32), here_mp * quarter, quarter, 0)
-    tiles = catalogue.reshape(catalogue.shape[0], catalogue.shape[1] // 128, 128)
     cat_grad, sums = step(
-        seq_for,
-        taken // seq_dev,
+        source,
+        lengths,
+        source.reshape(NX * NZ * NC, SEQ_DEV),
         owners.T,
         item_rows.T,
-        per_row.astype(F32)[:, None],
-        jnp.broadcast_to(valid[None, :], (8, quarter)),
         history,
-        tiles,
         catalogue,
         w_in,
         w_out,

time: 234 us -> 212 us (0.906)
  Pallas kernels: 215 us -> 201 us
  other arithmetic: 3.65 us -> 0 us
  local copies, waits for them, and re-layouts: 10.3 us -> 7.33 us
    pallas_call x1, Pallas kernels: 215 us -> 201 us  [step(): pl.pallas_call(step_kernel, out_shape=(sds((rows_cat, width), F32), sds((...]
    unnamed x2 -> x1, local copies, waits for them, and re-layouts: 5.63 us -> 3.16 us
    reduce_sum x3 -> x0, other arithmetic: 2.35 us -> none  [the longest x1 0.88 us: per_device(): jnp.sum(jnp.where(source[None, :] == my_seqs[:, None], places[None, :], 0...]
where the time goes in v3:
time: 212 us; the launch traced here: 209 us
  Pallas kernels  201 us (95%)
  local copies, waits for them, and re-layouts  7.33 us (3%)
    pallas_call x1, Pallas kernels, step(): pl.pallas_call(step_kernel, out_shape=(sds((rows_cat, width), F32), sds((...  201 us

profile of v3, /device:TPU:1, one launch (start us, length us, event | category | flops | bytes accessed | tf_op | source)
XLA Modules:
  0.0 209.1 jit_solution(17062684263140591162)
XLA Ops:
  0.6 1.4 reshape.9.source_ref
  2.0 201.2 %step.1 = (f32[512,1024]{1,0:T(8,128)}, f32[5,16,256]{2,1,0:T(8,128)}) custom-call(s32[1024]{0:T(1024)} %source_s.1, s32[1024]{0:T(1024)} %lengths_s.1, s32[64,16]{1,0:T(8,128)} %reshape.9.source_ref, s32[8,128]{1,0:T(8,128)} %bitcast.6, s32[8,128]{1,0:T(8,128)} %bitcast.7, bf16[16,32,256]{2,1,0:T(8,128)(2,1)} %history_hbm.1, bf16[512,1024]{1,0:T(8,128)(2,1)} %cat_hbm.1, ...), custom_call_target="tpu_custom_call" | custom-call | tf_op jit(solution)/shard_map/step/pallas_call | solution.py:613
  203.2 1.3 slice_bitcast_fusion
  204.5 1.5 slice.6
  206.0 3.2 %copy.12 = f32[512,1024]{1,0:T(8,128)} copy(f32[512,1024]{1,0:T(8,128)} %get-tuple-element.12) | data formatting | bytes 4194304

commit v4 on v3

--- a/solution.py
+++ b/solution.py
@@ -402,25 +402,40 @@
         coef_out[pl.ds(base, chips)] = coef.reshape(chips, 1, lanes)
     along = jnp.sum(unit * slope, axis=-1, keepdims=True)
     grad[...] = ((slope - unit * along) * inv_out).astype(BF16)
-    copies = [
-        pltpu.make_async_remote_copy(
-            src_ref=grad,
-            dst_ref=cot.at[own, :],
+    right, left = lax.rem(im + 1, nm), lax.rem(im + nm - 1, nm)
+
+    def cot_copy(i, src, dst, m):
+        return pltpu.make_async_remote_copy(
+            src_ref=src,
+            dst_ref=dst,
             send_sem=cot_sem.at[0, i],
             recv_sem=cot_sem.at[1, i],
-            device_id=(ix, iz, ic, p),
+            device_id=(ix, iz, ic, m),
             device_id_type=MESH,
         )
-        for i, p in enumerate(peers)
-    ]
-    for copy in copies:
-        copy.start()
+
+    def cot_half(m, i):
+        half = quarter // 2
+        return cot.at[pl.ds(pl.multiple_of(m * quarter + i * half, half), half), :]
+
+    to_right = cot_copy(0, grad, cot.at[own, :], right)
+    to_left = cot_copy(1, grad, cot.at[own, :], left)
+    to_right.start()
+    to_left.start()
     to_both(lambda core, k: push(coef_out, coef_in, coef_sem, core, chip_at(k)))
     serve_units(1, 0, chips, 1)
     coef_in[me] = coef_out[me]
     cot[own, :] = grad[...]
-    for copy in copies:
-        copy.wait()
+    to_right.wait_recv()
+    on_right = cot_copy(2, cot_half(left, 0), cot_half(left, 0), right)
+    on_right.start()
+    to_left.wait_recv()
+    on_left = cot_copy(3, cot_half(right, 1), cot_half(right, 1), left)
+    on_left.start()
+    on_right.wait()
+    on_left.wait()
+    to_right.wait_send()
+    to_left.wait_send()
 
     gated_cot[...] = lax.dot_general(
         cot[...], w_out[...], OVER_COLS, preferred_element_type=F32
@@ -499,6 +514,24 @@
             )
         )
         copies[-1].start()
+    finish(coef_in, coef_sem, 1, n - 1)
+    rows_cat = cat.shape[0]
+    row = lax.broadcasted_iota(jnp.int32, (chips, rows_cat), 1)
+    for p, base in enumerate(bases):
+        wanted = asked[pl.ds(base, chips)].reshape(chips, lanes)
+        coef = coef_in[pl.ds(base, chips)].reshape(chips, lanes)
+        for r in range(CAP):
+            b = coef[:, r + 8 : r + 9]
+            high = b.astype(BF16).astype(F32)
+            span = slice((p * CAP + r) * chips, (p * CAP + r + 1) * chips)
+            side[span, :] = jnp.where(
+                lane == 0, high, jnp.where(lane == 1, b - high, 0.0)
+            ).astype(BF16)
+            hot[span, :] = (wanted[:, r : r + 1] == row).astype(F32).astype(BF16)
+    both = lax.dot_general(hot[...], side[...], OVER_ROWS, preferred_element_type=F32)
+    b_row = both[:, 0:1] + both[:, 1:2]
+    for c in range(0, width, 256):
+        cat_grad_ref[:, c : c + 256] = -b_row * cat[:, c : c + 256].astype(F32)
     swaps[nx - 1].wait()
     held = parts[:, ix, :, ic].astype(F32) + land_c[:, ix].astype(F32)
     for i, copy in enumerate(copies):
@@ -520,44 +553,31 @@
         )
         copies[-1].start()
 
-    finish(coef_in, coef_sem, 1, n - 1)
-    rows_cat = cat.shape[0]
-    row = lax.broadcasted_iota(jnp.int32, (chips, rows_cat), 1)
-
     def catalogue_half(p):
         base = bases[p]
         finish(unit_in, unit_sem.at[p], 1, chips - 1 + p)
-        wanted = asked[pl.ds(base, chips)].reshape(chips, lanes)
         coef = coef_in[pl.ds(base, chips)].reshape(chips, lanes)
         half = slice(p * CAP * chips, (p + 1) * CAP * chips)
         for r in range(CAP):
             spread(unit_in, base, r)
             a = coef[:, r : r + 1]
-            b = coef[:, r + 8 : r + 9]
-            high = b.astype(BF16).astype(F32)
             span = slice((p * CAP + r) * chips, (p * CAP + r + 1) * chips)
             for c in range(chunks):
                 chunk = tall[pl.ds(c, chips, stride=chunks), :]
                 mat[span, c * lanes : (c + 1) * lanes] = (chunk * a).astype(BF16)
-            side[span, :] = jnp.where(
-                lane == 0, high, jnp.where(lane == 1, b - high, 0.0)
-            ).astype(BF16)
-            hot[span, :] = (wanted[:, r : r + 1] == row).astype(F32).astype(BF16)
-        both = lax.dot_general(hot[half, :], side[half, :], OVER_ROWS, preferred_element_type=F32)
-        b_row = both[:, 0:1] + both[:, 1:2]
         for c in range(0, width, 256):
             at = slice(c, c + 256)
-            res = lax.dot_general(hot[half, :], mat[half, at], OVER_ROWS, preferred_element_type=F32)
-            res = res - b_row * cat[:, at].astype(F32)
-            cat_grad_ref[:, at] = res if p == 0 else cat_grad_ref[:, at] + res
+            cat_grad_ref[:, at] += lax.dot_general(
+                hot[half, :], mat[half, at], OVER_ROWS, preferred_element_type=F32
+            )
 
     catalogue_half(0)
+    catalogue_half(1)
     held = stage_z[:, iz].astype(F32)
     for i, copy in enumerate(copies):
         copy.wait()
         held = held + land_z[i].astype(F32)
     sums_ref[...] = held
-    catalogue_half(1)
 
     finish(want_out, ids_sem, 0, n - 1)
     finish(hist_out, hist_sem, 0, n_dp - 1)
@@ -607,7 +627,7 @@
         V((5, NZ, rows_out, cols), BF16), V((NZ - 1, 5, rows_out, cols), BF16),
         V((CAP * n, rows_cat), BF16), V((CAP * n, 128), BF16),
         dma((2,)), dma((2,)), dma((NC, 2)), dma((NC, 2)), dma((2,)),
-        dma((2, NM - 1)), dma((2, NM - 1)), dma((2, NM - 1)),
+        dma((2, NM - 1)), dma((2, NM - 1)), dma((2, 4)),
         dma((2, NX)), dma((2, NX - 1)), dma((2, NZ - 1)),
     ]
     return pl.pallas_call(

time: 212 us -> 202 us (0.953); the launches traced: 209 us -> 202 us
  Pallas kernels: 201 us -> 194 us
    pallas_call x1, Pallas kernels: 201 us -> 194 us  [step(): pl.pallas_call(step_kernel, out_shape=(sds((rows_cat, width), F32), sds((...]
where the time goes in v4:
time: 202 us
  Pallas kernels  194 us (96%)
  local copies, waits for them, and re-layouts  7.33 us (4%)
    pallas_call x1, Pallas kernels, step(): pl.pallas_call(step_kernel, out_shape=(sds((rows_cat, width), F32), sds((...  194 us

profile of v4, /device:TPU:1, one launch (start us, length us, event | category | flops | bytes accessed | tf_op | source)
XLA Modules:
  0.0 202.1 jit_solution(2173229041915809834)
XLA Ops:
  0.6 1.4 reshape.9.source_ref
  2.0 194.1 %step.1 = (f32[512,1024]{1,0:T(8,128)}, f32[5,16,256]{2,1,0:T(8,128)}) custom-call(s32[1024]{0:T(1024)} %source_s.1, s32[1024]{0:T(1024)} %lengths_s.1, s32[64,16]{1,0:T(8,128)} %reshape.9.source_ref, s32[8,128]{1,0:T(8,128)} %bitcast.6, s32[8,128]{1,0:T(8,128)} %bitcast.7, bf16[16,32,256]{2,1,0:T(8,128)(2,1)} %history_hbm.1, bf16[512,1024]{1,0:T(8,128)(2,1)} %cat_hbm.1, ...), custom_call_target="tpu_custom_call" | custom-call | tf_op jit(solution)/shard_map/step/pallas_call | solution.py:633
  196.2 1.3 slice_bitcast_fusion
  197.5 1.5 slice.6
  199.0 3.2 %copy.12 = f32[512,1024]{1,0:T(8,128)} copy(f32[512,1024]{1,0:T(8,128)} %get-tuple-element.12) | data formatting | bytes 4194304

commit v5 on v4

--- a/solution.py
+++ b/solution.py
@@ -102,8 +102,8 @@
 def step_kernel(
     source_s, lengths_s, source_ref, owners_ref, rows_ref,
     history_hbm, cat_hbm, w_in_hbm, w_out_hbm,
-    cat_grad_ref, sums_ref,
-    count_ref, seq_v, seq_s, hist, hist_out, arrived, tiles, cat, w_in, w_out, load_sem,
+    cat_grad_hbm, sums_ref,
+    cat_grad_ref, store_sem, count_ref, seq_v, seq_s, hist, hist_out, arrived, tiles, cat, w_in, w_out, load_sem,
     want, event, rank, col, chosen_v, want_out, asked, asked_s, chosen_s, small_sem,
     fetch_out, fetch_in, unit_out, unit_in, coef_out, coef_in,
     part, flat, normed, preact, proj, gated, staged, landed,
@@ -169,7 +169,13 @@
     to_smem.start()
     from_here = lax.div(source_ref[...], SEQ_DEV) == here_dp
     local = jnp.where(from_here, lax.rem(source_ref[...], SEQ_DEV), 0)
-    local = jnp.max(local, axis=1, keepdims=True)
+    groups = 128 // SEQ_DEV
+    local = jnp.broadcast_to(
+        local.reshape(n_dp // groups, 1, 128), (n_dp // groups, groups, 128)
+    ).reshape(n_dp, 128)
+    at_row = lax.rem(lax.broadcasted_iota(jnp.int32, (n_dp, 128), 0), groups)
+    at_lane = lax.div(lax.broadcasted_iota(jnp.int32, (n_dp, 128), 1), SEQ_DEV)
+    local = jnp.max(jnp.where(at_row == at_lane, local, 0), axis=1, keepdims=True)
     seq_v[...] = jnp.broadcast_to(local, (n_dp, 128)).reshape(seq_v.shape)
     seq_copy = pltpu.make_async_copy(seq_v, seq_s, small_sem.at[1])
     seq_copy.start()
@@ -573,12 +579,15 @@
 
     catalogue_half(0)
     catalogue_half(1)
+    store = pltpu.make_async_copy(cat_grad_ref, cat_grad_hbm, store_sem)
+    store.start()
     held = stage_z[:, iz].astype(F32)
     for i, copy in enumerate(copies):
         copy.wait()
         held = held + land_z[i].astype(F32)
     sums_ref[...] = held
 
+    store.wait()
     finish(want_out, ids_sem, 0, n - 1)
     finish(hist_out, hist_sem, 0, n_dp - 1)
     for p in range(nc):
@@ -608,7 +617,7 @@
     anyw = pl.BlockSpec(memory_space=pl.ANY)
     message = (n, CAP, chunks, 128)
     scratch = [
-        V((rows_all, 1), F32), V((n_dp, 1, 128), I32), pltpu.SMEM((n_dp, 1, 128), I32),
+        V((rows_cat, width), F32), dma, V((rows_all, 1), F32), V((n_dp, 1, 128), I32), pltpu.SMEM((n_dp, 1, 128), I32),
         V(history.shape, BF16), V((n_dp, steps, cols), BF16), V((n_dp, steps, cols), BF16),
         V((rows_cat, chunks, 128), BF16), V(catalogue.shape, BF16), V(w_in.shape, BF16), V(w_out.shape, BF16), dma((4,)),
         V((n, 128), I32), V((n, 128), I32), V((n, quarter), I32), V((n, quarter), I32),
@@ -634,7 +643,7 @@
         step_kernel,
         out_shape=(sds((rows_cat, width), F32), sds((5, rows_out, cols), F32)),
         in_specs=[SM, SM, VM, VM, VM] + [anyw] * 4,
-        out_specs=(VM, VM),
+        out_specs=(anyw, VM),
         scratch_shapes=scratch,
         compiler_params=params(collective_id=0, has_side_effects=True),
         name="step",
@@ -645,7 +654,7 @@
     cat_grad, sums = step(
         source,
         lengths,
-        source.reshape(NX * NZ * NC, SEQ_DEV),
+        source.reshape(-1, 128),
         owners.T,
         item_rows.T,
         history,

time: 202 us -> 202 us (level)
  no operation moved by 1% of the time
where the time goes in v5:
time: 202 us
  Pallas kernels  195 us (97%)
  local copies, waits for them, and re-layouts  5.96 us (3%)
    pallas_call x1, Pallas kernels, step(): pl.pallas_call(step_kernel, out_shape=(sds((rows_cat, width), F32), sds((...  195 us

profile of v5, /device:TPU:1, one launch (start us, length us, event | category | flops | bytes accessed | tf_op | source)
XLA Modules:
  0.0 201.9 jit_solution(4157784478969757289)
XLA Ops:
  0.6 195.3 %step.1 = (f32[512,1024]{1,0:T(8,128)}, f32[5,16,256]{2,1,0:T(8,128)}) custom-call(s32[1024]{0:T(1024)} %source_s.1, s32[1024]{0:T(1024)} %lengths_s.1, s32[8,128]{1,0:T(8,128)} %bitcast.7, s32[8,128]{1,0:T(8,128)} %bitcast.8, s32[8,128]{1,0:T(8,128)} %bitcast.9, bf16[16,32,256]{2,1,0:T(8,128)(2,1)} %history_hbm.1, bf16[512,1024]{1,0:T(8,128)(2,1)} %cat_hbm.1, ...), custom_call_target="tpu_custom_call" | custom-call | tf_op jit(solution)/shard_map/step/pallas_call | solution.py:642
  195.9 1.3 slice_bitcast_fusion
  197.3 1.5 slice.6
  198.7 3.2 %copy.12 = f32[512,1024]{1,0:T(8,128)} copy(f32[512,1024]{1,0:T(8,128)} %get-tuple-element.12) | data formatting | bytes 4194304

commit v6 on v5

--- a/solution.py
+++ b/solution.py
@@ -102,7 +102,7 @@
 def step_kernel(
     source_s, lengths_s, source_ref, owners_ref, rows_ref,
     history_hbm, cat_hbm, w_in_hbm, w_out_hbm,
-    cat_grad_hbm, sums_ref,
+    cat_grad_hbm, w_in_sum, w_out_sum,
     cat_grad_ref, store_sem, count_ref, seq_v, seq_s, hist, hist_out, arrived, tiles, cat, w_in, w_out, load_sem,
     want, event, rank, col, chosen_v, want_out, asked, asked_s, chosen_s, small_sem,
     fetch_out, fetch_in, unit_out, unit_in, coef_out, coef_in,
@@ -585,7 +585,8 @@
     for i, copy in enumerate(copies):
         copy.wait()
         held = held + land_z[i].astype(F32)
-    sums_ref[...] = held
+    w_in_sum[...] = held[:4]
+    w_out_sum[...] = held[4]
 
     store.wait()
     finish(want_out, ids_sem, 0, n - 1)
@@ -641,9 +642,9 @@
     ]
     return pl.pallas_call(
         step_kernel,
-        out_shape=(sds((rows_cat, width), F32), sds((5, rows_out, cols), F32)),
+        out_shape=(sds((rows_cat, width), F32), sds((4, rows_out, cols), F32), sds((rows_out, cols), F32)),
         in_specs=[SM, SM, VM, VM, VM] + [anyw] * 4,
-        out_specs=(anyw, VM),
+        out_specs=(anyw, VM, VM),
         scratch_shapes=scratch,
         compiler_params=params(collective_id=0, has_side_effects=True),
         name="step",
@@ -651,7 +652,7 @@
 
 
 def per_device(history, lengths, source, owners, item_rows, catalogue, w_in, w_out):
-    cat_grad, sums = step(
+    cat_grad, w_in_grad, w_out_grad = step(
         source,
         lengths,
         source.reshape(-1, 128),
@@ -662,7 +663,7 @@
         w_in,
         w_out,
     )
-    return (sums[:4], sums[4].T, cat_grad)
+    return (w_in_grad, w_out_grad.T, cat_grad)
 
 
 def solution(mesh):

time: 202 us -> 202 us (level)
    unnamed x1 -> x3, local copies, waits for them, and re-layouts: 3.16 us -> 5.95 us
where the time goes in v6:
time: 202 us
  Pallas kernels  195 us (97%)
  local copies, waits for them, and re-layouts  5.95 us (3%)
    pallas_call x1, Pallas kernels, step(): pl.pallas_call(step_kernel, out_shape=(sds((rows_cat, width), F32), sds((...  195 us
    unnamed x3, local copies, waits for them, and re-layouts  5.95 us

profile of v6, /device:TPU:1, one launch (start us, length us, event | category | flops | bytes accessed | tf_op | source)
XLA Modules:
  0.0 202.0 jit_solution(5191141999833735343)
XLA Ops:
  0.6 195.4 %step.1 = (f32[512,1024]{1,0:T(8,128)}, f32[4,16,256]{2,1,0:T(8,128)}, f32[16,256]{1,0:T(8,128)}) custom-call(s32[1024]{0:T(1024)} %source_s.1, s32[1024]{0:T(1024)} %lengths_s.1, s32[8,128]{1,0:T(8,128)} %bitcast.4, s32[8,128]{1,0:T(8,128)} %bitcast.6, s32[8,128]{1,0:T(8,128)} %bitcast.7, bf16[16,32,256]{2,1,0:T(8,128)(2,1)} %history_hbm.1, ...), custom_call_target="tpu_custom_call" | custom-call | tf_op jit(solution)/shard_map/step/pallas_call | solution.py:643
  196.0 1.5 copy.14
  197.5 1.3 copy.15
  198.8 3.2 %copy.16 = f32[512,1024]{1,0:T(8,128)} copy(f32[512,1024]{1,0:T(8,128)} %get-tuple-element.14) | data formatting | bytes 4194304
